TPU v7x, 256 devices: a whole 4x4x8 slice. The times are simulated.
256 devices in a mesh: leaf: 32 (over z, y), head: 8 (over x, core).
Axes of the slice: x: 4, y: 4, z: 8, core: 2. Of those that a mesh axis runs over, the one named last changes fastest.
Arguments:
- query_in: bfloat16 [4096, 8192], P('leaf', 'head'), may hold values from -12 to 12
- key_in: bfloat16 [4096, 1024], P(('leaf', 'head')), may hold values from -12 to 12
- value_in: bfloat16 [4096, 1024], P(('leaf', 'head')), may hold values from -6 to 6
- out_grad: bfloat16 [4096, 8192], P('leaf', 'head'), may hold values from -6 to 6
- ancestry: int32 [32, 8], replicated, may hold values from -1 to 31, as said below
- node_len: int32 [32], replicated, may hold values from 64 to 128, as said below
Outputs:
- attended: bfloat16 [4096, 8192], P('leaf', 'head')
- query_grad: float32 [4096, 8192], P('leaf', 'head')
- key_grad: float32 [4096, 1024], P(('leaf', 'head'))
- value_grad: float32 [4096, 1024], P(('leaf', 'head'))
Inputs may be any that keep to these rules, and one draw needn't show every extreme that they name: `ancestry`: row g lists the ancestors of node g from the root, node 0, at column 0 down to node g itself at column depth(g), then -1; every ancestor of a node comes before it; nodes 0 to 3 form a chain. `node_len`: the root's length is 128, the last node's 128 // 2.
All inputs are finite; a program needn't handle non-finite values.
Results may differ from a plain program's by a relative error of at most 0.019.
Values may be sent and summed in bfloat16 or wider, within the bound.
No kernel may reach another device: no remote copies, remote signals or barrier semaphores. Data moves between devices by JAX's collectives and lax.ppermute only.
A program may use at most 64 MiB of HBM per device.

v0:
```python
import jax
import jax.numpy as jnp
from jax import lax
from jax.experimental import pallas as pl
from jax.experimental.pallas import tpu as pltpu
from jax.sharding import Mesh, PartitionSpec as P

QH = 64
KVH = 8
HD = 128
BLK = 128
ANC = 8
NODES = 32
GROUP = QH // KVH
FAR = 4
NEAR = 8
PIECE = 4
SHARE = KVH * PIECE
QUADS = 16 // PIECE
WIDE = GROUP * BLK
STRIP = 256
LOG2E = 1.4426950408889634
SCALE = HD ** (-0.5)
LOW = -1e30

NT = (((1,), (1,)), ((), ()))
NN = (((1,), (0,)), ((), ()))


def dot(a, b, dims=NN):
    return lax.dot_general(a, b, dims, preferred_element_type=jnp.float32)


def cut_kernel(key_ref, value_ref, out_ref):
    for kind, ref in ((0, key_ref), (1, value_ref)):
        rows = ref[...].astype(jnp.float32)
        for quad in range(QUADS):
            part = rows[quad * PIECE : (quad + 1) * PIECE]
            share = jnp.concatenate([part[:, h * HD : (h + 1) * HD] for h in range(KVH)], axis=0)
            share = share.astype(jnp.bfloat16)
            for f in range(FAR):
                first = (f * NEAR + quad * 2 + kind) * SHARE
                out_ref[first : first + SHARE, :] = share


def prep_kernel(q_ref, g_ref, out_ref):
    for h in range(GROUP):
        here = slice(h * HD, (h + 1) * HD)
        g = g_ref[:, here]
        for part, block in enumerate((q_ref[:, here], g, g.T)):
            first = part * WIDE + h * BLK
            out_ref[first : first + BLK, :] = block


def pick_kernel(leaf_ref, anc_ref, rows_ref, out_ref, sem):
    base = (leaf_ref[0] // NEAR) * NEAR
    for j in range(NEAR):
        for s in range(ANC):
            node = jnp.maximum(anc_ref[s, base + j], 0)
            first = pl.multiple_of(node * SHARE, SHARE)
            to = out_ref.at[pl.ds((j * ANC + s) * SHARE, SHARE), :]
            pltpu.make_async_copy(rows_ref.at[pl.ds(first, SHARE), :], to, sem).start()
    pltpu.make_async_copy(out_ref, out_ref, sem).wait()


def add_kernel(leaf_ref, anc_ref, terms_ref, out_ref, even_ref, odd_ref):
    base = (leaf_ref[0] // NEAR) * NEAR

    def term(j, s):
        first = (j * ANC + s) * SHARE
        return terms_ref[first : first + SHARE, :].astype(jnp.float32)

    root = term(0, 0)
    for j in range(1, NEAR):
        root = root + term(j, 0)
    even_ref[:SHARE, :] = root
    even_ref[SHARE:, :] = jnp.zeros_like(even_ref[SHARE:, :])
    odd_ref[...] = jnp.zeros_like(odd_ref)
    for s in range(1, ANC):
        nodes = [anc_ref[s, base + j] for j in range(NEAR)]
        highest = nodes[0]
        for node in nodes[1:]:
            highest = jnp.maximum(highest, node)

        @pl.when(highest >= 0)
        def _():
            for j, node in enumerate(nodes):
                ref = odd_ref if j % 2 else even_ref
                place = jnp.where(node >= 0, node, NODES)
                here = pl.ds(pl.multiple_of(place * SHARE, SHARE), SHARE)
                ref[here, :] = ref[here, :] + term(j, s)

    rows = NODES * SHARE
    out_ref[...] = (even_ref[:rows, :] + odd_ref[:rows, :]).astype(jnp.bfloat16)


def finish_kernel(back_ref, key_ref, value_ref):
    part = NEAR * SHARE
    total = back_ref[:part, :].astype(jnp.float32)
    for f in range(1, FAR):
        total = total + back_ref[f * part : (f + 1) * part, :].astype(jnp.float32)
    for kind, ref in ((0, key_ref), (1, value_ref)):
        for h in range(KVH):
            rows = []
            for quad in range(QUADS):
                first = (quad * 2 + kind) * SHARE + h * PIECE
                rows.append(total[first : first + PIECE])
            ref[:, h * HD : (h + 1) * HD] = jnp.concatenate(rows, axis=0)


def keys_of(kv_ref, s, kind):
    firsts = [((2 * quad + kind) * ANC + s) * SHARE for quad in range(QUADS)]
    return jnp.concatenate([kv_ref[pl.ds(pl.multiple_of(f, SHARE), SHARE), :] for f in firsts], axis=0)


def used_slots(anc_ref, leaf):
    used = jnp.int32(0)
    for s in range(ANC):
        used = used + jnp.where(anc_ref[s, leaf] >= 0, 1, 0)
    return used


STRIPS = [slice(i * STRIP, (i + 1) * STRIP) for i in range(WIDE // STRIP)]


def attention_kernel(
    leaf_ref, anc_ref, len_ref, in_ref, kv_ref, kvg_ref, dl_ref, out_ref,
    e_ref, top_ref, sum_ref, acc_ref,
):
    leaf = leaf_ref[0]
    used = used_slots(anc_ref, leaf)

    def stacked(part, strip):
        return in_ref[part * WIDE + strip.start : part * WIDE + strip.stop, :]

    def turned(strip):
        rows = stacked(2, strip)
        return jnp.concatenate([rows[i * HD : (i + 1) * HD] for i in range(STRIP // BLK)], axis=1)

    top_ref[...] = jnp.full_like(top_ref, LOW)
    sum_ref[...] = jnp.zeros_like(sum_ref)
    acc_ref[...] = jnp.zeros_like(acc_ref)

    row = lax.broadcasted_iota(jnp.int32, (BLK, BLK), 0)
    place = ((row // PIECE) % KVH) * 16 + (row // SHARE) * PIECE + row % PIECE
    query = lax.broadcasted_iota(jnp.int32, (BLK, BLK), 1)

    def logits_pass(s, carry):
        node = anc_ref[s, leaf]
        length = len_ref[node]
        ends = jnp.where(node == leaf, jnp.minimum(query + 1, length), length)
        seen = jnp.concatenate([place < ends] * (STRIP // BLK), axis=1)
        key = keys_of(kv_ref, s, 0)
        for strip in STRIPS:
            raw = dot(key, stacked(0, strip), NT) * (SCALE * LOG2E)
            raw = jnp.where(seen, raw, LOW)
            e_ref[s, :, strip] = raw
            high = jnp.max(raw.reshape(BLK // 8, 8, STRIP), axis=0)
            top_ref[:, strip] = jnp.maximum(top_ref[:, strip], high)
        return carry

    lax.fori_loop(0, used, logits_pass, 0)
    top_ref[...] = jnp.broadcast_to(jnp.max(top_ref[...], axis=0, keepdims=True), top_ref.shape)

    def output_pass(s, carry):
        value_t = keys_of(kv_ref, s, 1).T
        for strip in STRIPS:
            expo = jnp.exp2(e_ref[s, :, strip] - top_ref[:1, strip])
            e_ref[s, :, strip] = expo
            sum_ref[:, strip] = sum_ref[:, strip] + jnp.sum(expo.reshape(BLK // 8, 8, STRIP), axis=0)
            acc_ref[:, strip] = acc_ref[:, strip] + dot(value_t, expo.astype(jnp.bfloat16))
        return carry

    lax.fori_loop(0, used, output_pass, 0)
    for strip in STRIPS:
        inverse = 1.0 / jnp.sum(sum_ref[:, strip], axis=0, keepdims=True)
        out_t = (acc_ref[:, strip] * inverse).astype(jnp.bfloat16)
        delta = jnp.sum(turned(strip).astype(jnp.float32) * out_t.astype(jnp.float32), axis=0, keepdims=True)
        top_ref[:1, strip] = inverse
        sum_ref[:1, strip] = delta
        out_ref[:, strip] = out_t

    def gradient_pass(s, carry):
        value = keys_of(kv_ref, s, 1)
        key_sum = jnp.zeros((BLK, HD), jnp.float32)
        value_sum = jnp.zeros((BLK, HD), jnp.float32)
        for strip in STRIPS:
            dprob = dot(value, turned(strip))
            weights = e_ref[s, :, strip] * top_ref[:1, strip]
            dlogit = (weights * (dprob - sum_ref[:1, strip])).astype(jnp.bfloat16)
            value_sum = value_sum + dot(weights.astype(jnp.bfloat16), stacked(1, strip))
            key_sum = key_sum + dot(dlogit, stacked(0, strip))
            dl_ref[s, :, strip] = dlogit
        for kind, total in ((0, key_sum * SCALE), (1, value_sum)):
            total = total.astype(jnp.bfloat16)
            for quad in range(QUADS):
                first = pl.multiple_of(((2 * quad + kind) * ANC + s) * SHARE, SHARE)
                kvg_ref[pl.ds(first, SHARE), :] = total[quad * SHARE : (quad + 1) * SHARE]
        return carry

    lax.fori_loop(0, used, gradient_pass, 0)

def late_kernel(leaf_ref, anc_ref, kv_ref, dl_ref, out_t_ref, out_ref, qg_ref, acc_ref):
    used = used_slots(anc_ref, leaf_ref[0])
    for h in range(GROUP):
        here = slice(h * BLK, (h + 1) * BLK)
        out_ref[:, here] = out_t_ref[:, here].T
    acc_ref[...] = jnp.zeros_like(acc_ref)

    def query_pass(s, carry):
        key_t = keys_of(kv_ref, s, 0).T
        for strip in STRIPS:
            acc_ref[:, strip] = acc_ref[:, strip] + dot(key_t, dl_ref[s, :, strip])
        return carry

    lax.fori_loop(0, used, query_pass, 0)
    for h in range(GROUP):
        here = slice(h * BLK, (h + 1) * BLK)
        qg_ref[:, here] = (acc_ref[:, here] * SCALE).T


def near_memory(x):
    return pltpu.with_memory_space_constraint(x, pltpu.VMEM)


SMEM = pl.BlockSpec(memory_space=pltpu.SMEM)
VMEM = pl.BlockSpec(memory_space=pltpu.VMEM)


ANY = pl.BlockSpec(memory_space=pl.ANY)


def room(mebibytes):
    return pltpu.CompilerParams(vmem_limit_bytes=mebibytes << 20)


def shaped(shape, dtype):
    return jax.ShapeDtypeStruct(shape, dtype)


def per_device(query_in, key_in, value_in, out_grad, ancestry, node_len):
    everyone = ("far", "near", "head")
    leaf = (lax.axis_index("far") * NEAR + lax.axis_index("near")).astype(jnp.int32).reshape(1)
    ancestry_t = ancestry.T
    rows = key_in.shape[0]

    low, wide = jnp.bfloat16, jnp.float32
    pieces = pl.pallas_call(
        cut_kernel,
        out_shape=shaped((FAR * NEAR * SHARE, HD), low),
        in_specs=[VMEM, VMEM],
        out_specs=VMEM,
        compiler_params=room(4),
        name="cut",
    )(key_in, value_in)
    shares = lax.all_to_all(pieces, everyone, split_axis=0, concat_axis=0, tiled=True)
    stacked = pl.pallas_call(
        prep_kernel,
        out_shape=pltpu.VMEM((3 * WIDE, HD), low),
        in_specs=[VMEM, VMEM],
        out_specs=VMEM,
        compiler_params=room(4),
        name="prep",
    )(query_in, out_grad)
    picked = pl.pallas_call(
        pick_kernel,
        out_shape=shaped((NEAR * ANC * SHARE, HD), low),
        in_specs=[SMEM, SMEM, VMEM],
        out_specs=ANY,
        scratch_shapes=[pltpu.SemaphoreType.DMA],
        compiler_params=room(4),
        name="pick",
    )(leaf, ancestry_t, near_memory(shares))
    kv = near_memory(lax.all_to_all(picked, "near", split_axis=0, concat_axis=0, tiled=True))
    terms, dlogit, out_t = pl.pallas_call(
        attention_kernel,
        out_shape=(
            shaped((2 * ANC * BLK, HD), low),
            pltpu.VMEM((ANC, BLK, WIDE), low),
            pltpu.VMEM((HD, WIDE), low),
        ),
        in_specs=[SMEM, SMEM, SMEM, VMEM, VMEM],
        out_specs=(VMEM, VMEM, VMEM),
        scratch_shapes=[
            pltpu.VMEM((ANC, BLK, WIDE), wide),
            pltpu.VMEM((8, WIDE), wide),
            pltpu.VMEM((8, WIDE), wide),
            pltpu.VMEM((HD, WIDE), wide),
        ],
        compiler_params=room(16),
        name="attend",
    )(leaf, ancestry_t, node_len, near_memory(stacked), kv)
    terms = lax.all_to_all(terms, "near", split_axis=0, concat_axis=0, tiled=True)
    attended, query_grad = pl.pallas_call(
        late_kernel,
        out_shape=(shaped((BLK, GROUP * HD), low), shaped((BLK, GROUP * HD), wide)),
        in_specs=[SMEM, SMEM, VMEM, VMEM, VMEM],
        out_specs=(VMEM, VMEM),
        scratch_shapes=[pltpu.VMEM((HD, WIDE), wide)],
        compiler_params=room(8),
        name="late",
    )(leaf, ancestry_t, kv, near_memory(dlogit), near_memory(out_t))
    summed = pl.pallas_call(
        add_kernel,
        out_shape=shaped((NODES * SHARE, HD), low),
        in_specs=[SMEM, SMEM, VMEM],
        out_specs=VMEM,
        scratch_shapes=[
            pltpu.VMEM(((NODES + 1) * SHARE, HD), wide),
            pltpu.VMEM(((NODES + 1) * SHARE, HD), wide),
        ],
        compiler_params=room(8),
        name="add",
    )(leaf, ancestry_t, near_memory(terms))
    back = lax.all_to_all(summed, everyone, split_axis=0, concat_axis=0, tiled=True)
    key_grad, value_grad = pl.pallas_call(
        finish_kernel,
        out_shape=(shaped((rows, KVH * HD), wide), shaped((rows, KVH * HD), wide)),
        in_specs=[VMEM],
        out_specs=(VMEM, VMEM),
        compiler_params=room(8),
        name="finish",
    )(near_memory(back))
    return (attended, query_grad, key_grad, value_grad)


def solution(mesh):
    mesh = Mesh(mesh.devices.reshape(FAR, NEAR, KVH), ("far", "near", "head"))
    leaf = ("far", "near")
    token = ("far", "near", "head")
    return jax.shard_map(
        per_device,
        mesh=mesh,
        in_specs=(P(leaf, "head"), P(token, None), P(token, None), P(leaf, "head"), P(), P()),
        out_specs=(P(leaf, "head"), P(leaf, "head"), P(token, None), P(token, None)),
        check_vma=False,
    )
```

profile of v0, /device:TPU:1, one launch (start us, length us, event | category | flops | bytes accessed | tf_op | source)
XLA Modules:
  0.0 91.5 jit_solution(7510018670708029392)
XLA Ops:
  0.6 0.0 copy-start.5
  0.6 0.0 copy-start.1
  0.7 0.0 copy-start
  0.7 0.0 copy-start.6
  0.7 0.8 copy-done.6
  1.5 0.0 copy-start.7
  1.5 0.8 copy-done.7
  2.2 0.0 copy-start.8
  2.2 0.7 cut.1
  3.0 15.6 %all-to-all-start = ((bf16[256,4,128]{2,1,0:T(4,128)(2,1)}), bf16[256,4,128]{2,1,0:T(4,128)(2,1)S(1)}, u32[]{:S(2)}, u32[]{:S(2)}) async-start(bf16[256,4,128]{2,1,0:T(4,128)(2,1)} %bitcast.2), calls=%async_computation | async-start | bytes 524288 | tf_op jit(solution)/shard_map/all_to_all | solution.py:256
  18.6 15.3 %all-to-all-done = bf16[256,4,128]{2,1,0:T(4,128)(2,1)S(1)} async-done(((bf16[256,4,128]{2,1,0:T(4,128)(2,1)}), bf16[256,4,128]{2,1,0:T(4,128)(2,1)S(1)}, u32[]{:S(2)}, u32[]{:S(2)}) %all-to-all-start) | async-done | bytes 262176 | tf_op jit(solution)/shard_map/all_to_all | solution.py:256
  33.9 0.0 copy-start.4
  33.9 0.7 copy-done.4
  34.6 1.5 %pick.1 = bf16[2048,128]{1,0:T(8,128)(2,1)} custom-call(s32[1]{0:T(128)} %bitcast.leaf_ref, s32[8,32]{1,0:T(8,128)S(1)} %bitcast.16, bf16[1024,128]{1,0:T(8,128)(2,1)S(1)} %bitcast.14), custom_call_target="tpu_custom_call" | custom-call | tf_op jit(solution)/shard_map/pick/pallas_call | solution.py:265
  36.1 3.5 %all-to-all-start.1 = ((bf16[8,256,128]{2,1,0:T(8,128)(2,1)}), bf16[8,256,128]{2,1,0:T(8,128)(2,1)S(1)}, u32[]{:S(2)}, u32[]{:S(2)}) async-start(bf16[8,256,128]{2,1,0:T(8,128)(2,1)} %bitcast.4), calls=%async_computation.1 | async-start | bytes 1048576 | tf_op jit(solution)/shard_map/all_to_all | solution.py:274
  39.6 0.0 copy-done.1
  39.6 0.0 copy-done
  39.6 0.1 prep.1.in_ref
  39.7 7.8 %all-to-all-done.1 = bf16[8,256,128]{2,1,0:T(8,128)(2,1)S(1)} async-done(((bf16[8,256,128]{2,1,0:T(8,128)(2,1)}), bf16[8,256,128]{2,1,0:T(8,128)(2,1)S(1)}, u32[]{:S(2)}, u32[]{:S(2)}) %all-to-all-start.1) | async-done | bytes 524320 | tf_op jit(solution)/shard_map/all_to_all | solution.py:274
  47.6 0.0 copy-done.5
  47.6 0.0 copy-done.8
  47.6 1.8 %attend.1 = (bf16[2048,128]{1,0:T(8,128)(2,1)S(1)}, bf16[8,128,1024]{2,1,0:T(8,128)(2,1)S(1)}, bf16[128,1024]{1,0:T(8,128)(2,1)S(1)}) custom-call(s32[1]{0:T(128)} %bitcast.leaf_ref, s32[8,32]{1,0:T(8,128)S(1)} %bitcast.17, s32[32]{0:T(128)S(1)} %copy-done.8, bf16[3072,128]{1,0:T(8,128)(2,1)S(1)} %prep.1.in_ref, bf16[2048,128]{1,0:T(8,128)(2,1)S(1)} %bitcast.10), custom_call_target="tpu_custom_call" | custom-call | tf_op jit(solution)/shard_map/attend/pallas_call | solution.py:275
  49.4 0.0 copy-start.2
  49.4 14.1 %all_to_all.44 = bf16[8,256,128]{2,1,0:T(8,128)(2,1)S(1)} all-to-all(bf16[8,256,128]{2,1,0:T(8,128)(2,1)S(1)} %bitcast.15), channel_id=1, replica_groups=mesh['far'=4,'near'=8,'head'=8] {'near'}, dimensions={0} | all-to-all | bytes 1048576 | tf_op jit(solution)/shard_map/all_to_all | solution.py:293
  63.5 1.6 %add.5 = bf16[1024,128]{1,0:T(8,128)(2,1)} custom-call(s32[1]{0:T(128)} %bitcast.leaf_ref, s32[8,32]{1,0:T(8,128)S(1)} %bitcast.18, bf16[2048,128]{1,0:T(8,128)(2,1)S(1)} %bitcast.12), custom_call_target="tpu_custom_call" | custom-call | tf_op jit(solution)/shard_map/add/pallas_call | solution.py:303
  65.1 0.0 copy-done.2
  65.1 10.5 %all-to-all-start.3 = ((bf16[256,4,128]{2,1,0:T(4,128)(2,1)}), bf16[256,4,128]{2,1,0:T(4,128)(2,1)S(1)}, u32[]{:S(2)}, u32[]{:S(2)}) async-start(bf16[256,4,128]{2,1,0:T(4,128)(2,1)} %bitcast.8), calls=%async_computation.3 | async-start | bytes 524288 | tf_op jit(solution)/shard_map/all_to_all | solution.py:315
  75.5 0.0 copy-start.3
  75.5 0.9 %copy-done.3 = bf16[128,1024]{1,0:T(8,128)(2,1)S(1)} copy-done((bf16[128,1024]{1,0:T(8,128)(2,1)S(1)}, bf16[128,1024]{1,0:T(8,128)(2,1)}, u32[]{:S(2)}) %copy-start.3) | copy-done | bytes 262168
  76.5 2.0 %late.1 = (bf16[128,1024]{1,0:T(8,128)(2,1)}, f32[128,1024]{1,0:T(8,128)}) custom-call(s32[1]{0:T(128)} %bitcast.leaf_ref, s32[8,32]{1,0:T(8,128)S(1)} %bitcast.19, bf16[2048,128]{1,0:T(8,128)(2,1)S(1)} %bitcast.11, bf16[8,128,1024]{2,1,0:T(8,128)(2,1)S(1)} %get-tuple-element.11.dl_ref, bf16[128,1024]{1,0:T(8,128)(2,1)S(1)} %copy-done.3), custom_call_target="tpu_custom_call" | custom-call | tf_op jit(solution)/shard_map/late/pallas_call | solution.py:294
  78.5 12.4 %all-to-all-done.3 = bf16[256,4,128]{2,1,0:T(4,128)(2,1)S(1)} async-done(((bf16[256,4,128]{2,1,0:T(4,128)(2,1)}), bf16[256,4,128]{2,1,0:T(4,128)(2,1)S(1)}, u32[]{:S(2)}, u32[]{:S(2)}) %all-to-all-start.3) | async-done | bytes 262176 | tf_op jit(solution)/shard_map/all_to_all | solution.py:315
  90.8 0.7 finish.1
Async XLA Ops:
  0.6 46.9 %copy-start.5 = (s32[32,8]{0,1:T(8,128)S(1)}, s32[32,8]{0,1:T(8,128)}, u32[]{:S(2)}) copy-start(s32[32,8]{0,1:T(8,128)} %param.10) | copy-start | bytes 3076
  0.6 38.9 %copy-start.1 = (bf16[128,1024]{1,0:T(8,128)(2,1)S(1)}, bf16[128,1024]{1,0:T(8,128)(2,1)}, u32[]{:S(2)}) copy-start(bf16[128,1024]{1,0:T(8,128)(2,1)} %g_ref.1) | copy-start | bytes 786436
  0.7 38.9 %copy-start = (bf16[128,1024]{1,0:T(8,128)(2,1)S(1)}, bf16[128,1024]{1,0:T(8,128)(2,1)}, u32[]{:S(2)}) copy-start(bf16[128,1024]{1,0:T(8,128)(2,1)} %q_ref.1) | copy-start | bytes 786436
  0.7 0.8 copy-start.6
  1.5 0.8 copy-start.7
  2.2 45.3 %copy-start.8 = (s32[32]{0:T(128)S(1)}, s32[32]{0:T(128)}, u32[]{:S(2)}) copy-start(s32[32]{0:T(128)} %len_ref.1) | copy-start | bytes 388
  3.0 30.9 %all-to-all-start = ((bf16[256,4,128]{2,1,0:T(4,128)(2,1)}), bf16[256,4,128]{2,1,0:T(4,128)(2,1)S(1)}, u32[]{:S(2)}, u32[]{:S(2)}) async-start(bf16[256,4,128]{2,1,0:T(4,128)(2,1)} %bitcast.2), calls=%async_computation | async-start | bytes 524288 | tf_op jit(solution)/shard_map/all_to_all | solution.py:256
  33.9 0.7 copy-start.4
  36.1 11.5 %all-to-all-start.1 = ((bf16[8,256,128]{2,1,0:T(8,128)(2,1)}), bf16[8,256,128]{2,1,0:T(8,128)(2,1)S(1)}, u32[]{:S(2)}, u32[]{:S(2)}) async-start(bf16[8,256,128]{2,1,0:T(8,128)(2,1)} %bitcast.4), calls=%async_computation.1 | async-start | bytes 1048576 | tf_op jit(solution)/shard_map/all_to_all | solution.py:274
  49.4 15.7 %copy-start.2 = (bf16[128,1024]{1,0:T(8,128)(2,1)}, bf16[128,1024]{1,0:T(8,128)(2,1)S(1)}, u32[]{:S(2)}) copy-start(bf16[128,1024]{1,0:T(8,128)(2,1)S(1)} %get-tuple-element.12.out_t_ref) | copy-start | bytes 786436
  65.1 25.8 %all-to-all-start.3 = ((bf16[256,4,128]{2,1,0:T(4,128)(2,1)}), bf16[256,4,128]{2,1,0:T(4,128)(2,1)S(1)}, u32[]{:S(2)}, u32[]{:S(2)}) async-start(bf16[256,4,128]{2,1,0:T(4,128)(2,1)} %bitcast.8), calls=%async_computation.3 | async-start | bytes 524288 | tf_op jit(solution)/shard_map/all_to_all | solution.py:315
  75.5 1.0 %copy-start.3 = (bf16[128,1024]{1,0:T(8,128)(2,1)S(1)}, bf16[128,1024]{1,0:T(8,128)(2,1)}, u32[]{:S(2)}) copy-start(bf16[128,1024]{1,0:T(8,128)(2,1)} %copy-done.2) | copy-start | bytes 786436
where the time goes:
time: 91.9 us; the launch traced here: 91.5 us
  waiting for transfers between devices  35.5 us (39%)
  starting transfers between devices  29.6 us (32%)
  blocking collectives  14.1 us (15%)
  Pallas kernels  8.39 us (9%)
  local copies, waits for them, and re-layouts  3.22 us (4%)
    all_to_all x1, starting transfers between devices, per_device(): lax.all_to_all(pieces, everyone, split_axis=0, concat_axis=0, tiled=True)  15.6 us
    all_to_all x1, waiting for transfers between devices, per_device(): lax.all_to_all(pieces, everyone, split_axis=0, concat_axis=0, tiled=True)  15.3 us
    all_to_all x1, blocking collectives, per_device(): lax.all_to_all(terms, 'near', split_axis=0, concat_axis=0, tiled=True)  14.1 us
    all_to_all x1, waiting for transfers between devices, per_device(): lax.all_to_all(summed, everyone, split_axis=0, concat_axis=0, tiled=True)  12.4 us
    all_to_all x1, starting transfers between devices, per_device(): lax.all_to_all(summed, everyone, split_axis=0, concat_axis=0, tiled=True)  10.5 us
    all_to_all x1, waiting for transfers between devices, per_device(): lax.all_to_all(picked, 'near', split_axis=0, concat_axis=0, tiled=True)  7.82 us
    all_to_all x1, starting transfers between devices, per_device(): lax.all_to_all(picked, 'near', split_axis=0, concat_axis=0, tiled=True)  3.51 us
    unnamed x18, local copies, waits for them, and re-layouts  3.22 us
  transfers between devices with their start and end apart: 3, of which 3 were waited for; matrix products, arithmetic and copies ran while one was open for 0% of the time, Pallas kernels for 2%

commit v1 on v0

--- a/solution.py
+++ b/solution.py
@@ -31,8 +31,12 @@
     return lax.dot_general(a, b, dims, preferred_element_type=jnp.float32)
 
 
-def cut_kernel(key_ref, value_ref, out_ref):
-    for kind, ref in ((0, key_ref), (1, value_ref)):
+def cut_kernel(key_hbm, value_hbm, out_ref, key_ref, value_ref, sems):
+    kinds = ((key_hbm, key_ref), (value_hbm, value_ref))
+    for kind, (far_ref, ref) in enumerate(kinds):
+        pltpu.make_async_copy(far_ref, ref, sems.at[kind]).start()
+    for kind, (far_ref, ref) in enumerate(kinds):
+        pltpu.make_async_copy(far_ref, ref, sems.at[kind]).wait()
         rows = ref[...].astype(jnp.float32)
         for quad in range(QUADS):
             part = rows[quad * PIECE : (quad + 1) * PIECE]
@@ -52,20 +56,36 @@
             out_ref[first : first + BLK, :] = block
 
 
-def pick_kernel(leaf_ref, anc_ref, rows_ref, out_ref, sem):
+def levels_of(leaf_ref, anc_ref):
     base = (leaf_ref[0] // NEAR) * NEAR
-    for j in range(NEAR):
-        for s in range(ANC):
-            node = jnp.maximum(anc_ref[s, base + j], 0)
-            first = pl.multiple_of(node * SHARE, SHARE)
-            to = out_ref.at[pl.ds((j * ANC + s) * SHARE, SHARE), :]
-            pltpu.make_async_copy(rows_ref.at[pl.ds(first, SHARE), :], to, sem).start()
-    pltpu.make_async_copy(out_ref, out_ref, sem).wait()
+    for s in range(ANC):
+        nodes = [anc_ref[s, base + j] for j in range(NEAR)]
+        highest = nodes[0]
+        for node in nodes[1:]:
+            highest = jnp.maximum(highest, node)
+        yield s, nodes, highest >= 0
+
+
+def pick_kernel(leaf_ref, anc_ref, rows_ref, out_ref, sems):
+    levels = list(levels_of(leaf_ref, anc_ref))
+    for s, nodes, some in levels:
+
+        @pl.when(some)
+        def _():
+            for j, node in enumerate(nodes):
+                first = pl.multiple_of(jnp.maximum(node, 0) * SHARE, SHARE)
+                to = out_ref.at[pl.ds((j * ANC + s) * SHARE, SHARE), :]
+                pltpu.make_async_copy(rows_ref.at[pl.ds(first, SHARE), :], to, sems.at[s]).start()
+
+    for s, nodes, some in levels:
+
+        @pl.when(some)
+        def _():
+            block = out_ref.at[: NEAR * SHARE, :]
+            pltpu.make_async_copy(block, block, sems.at[s]).wait()
 
 
 def add_kernel(leaf_ref, anc_ref, terms_ref, out_ref, even_ref, odd_ref):
-    base = (leaf_ref[0] // NEAR) * NEAR
-
     def term(j, s):
         first = (j * ANC + s) * SHARE
         return terms_ref[first : first + SHARE, :].astype(jnp.float32)
@@ -76,13 +96,11 @@
     even_ref[:SHARE, :] = root
     even_ref[SHARE:, :] = jnp.zeros_like(even_ref[SHARE:, :])
     odd_ref[...] = jnp.zeros_like(odd_ref)
-    for s in range(1, ANC):
-        nodes = [anc_ref[s, base + j] for j in range(NEAR)]
-        highest = nodes[0]
-        for node in nodes[1:]:
-            highest = jnp.maximum(highest, node)
-
-        @pl.when(highest >= 0)
+    for s, nodes, some in levels_of(leaf_ref, anc_ref):
+        if s == 0:
+            continue
+
+        @pl.when(some)
         def _():
             for j, node in enumerate(nodes):
                 ref = odd_ref if j % 2 else even_ref
@@ -223,11 +241,16 @@
     return pltpu.with_memory_space_constraint(x, pltpu.VMEM)
 
 
+def far_memory(x):
+    return pltpu.with_memory_space_constraint(x, pltpu.HBM)
+
+
 SMEM = pl.BlockSpec(memory_space=pltpu.SMEM)
 VMEM = pl.BlockSpec(memory_space=pltpu.VMEM)
 
 
 ANY = pl.BlockSpec(memory_space=pl.ANY)
+HBM = pl.BlockSpec(memory_space=pltpu.HBM)
 
 
 def room(mebibytes):
@@ -241,18 +264,23 @@
 def per_device(query_in, key_in, value_in, out_grad, ancestry, node_len):
     everyone = ("far", "near", "head")
     leaf = (lax.axis_index("far") * NEAR + lax.axis_index("near")).astype(jnp.int32).reshape(1)
-    ancestry_t = ancestry.T
+    ancestry_t, node_len = far_memory(ancestry.T), far_memory(node_len)
     rows = key_in.shape[0]
 
     low, wide = jnp.bfloat16, jnp.float32
     pieces = pl.pallas_call(
         cut_kernel,
         out_shape=shaped((FAR * NEAR * SHARE, HD), low),
-        in_specs=[VMEM, VMEM],
+        in_specs=[HBM, HBM],
         out_specs=VMEM,
+        scratch_shapes=[
+            pltpu.VMEM(key_in.shape, low),
+            pltpu.VMEM(key_in.shape, low),
+            pltpu.SemaphoreType.DMA((2,)),
+        ],
         compiler_params=room(4),
         name="cut",
-    )(key_in, value_in)
+    )(far_memory(key_in), far_memory(value_in))
     shares = lax.all_to_all(pieces, everyone, split_axis=0, concat_axis=0, tiled=True)
     stacked = pl.pallas_call(
         prep_kernel,
@@ -267,7 +295,7 @@
         out_shape=shaped((NEAR * ANC * SHARE, HD), low),
         in_specs=[SMEM, SMEM, VMEM],
         out_specs=ANY,
-        scratch_shapes=[pltpu.SemaphoreType.DMA],
+        scratch_shapes=[pltpu.SemaphoreType.DMA((ANC,))],
         compiler_params=room(4),
         name="pick",
     )(leaf, ancestry_t, near_memory(shares))

time: 91.9 us -> 90.7 us (0.987)
  starting transfers between devices: 29.6 us -> 26.5 us
  blocking collectives: 14.1 us -> 16.9 us
  local copies, waits for them, and re-layouts: 3.22 us -> 0.96 us
  Pallas kernels: 8.39 us -> 9.77 us
    all_to_all x1, starting transfers between devices: 10.5 us -> 7.3 us  [per_device(): lax.all_to_all(summed, everyone, split_axis=0, concat_axis=0, tiled=True)]
    all_to_all x1, blocking collectives: 14.1 us -> 16.9 us  [per_device(): lax.all_to_all(terms, 'near', split_axis=0, concat_axis=0, tiled=True)]
    unnamed x18 -> x8, local copies, waits for them, and re-layouts: 3.22 us -> 0.96 us
where the time goes in v1:
time: 90.7 us; the launch traced here: 90.3 us
  waiting for transfers between devices  35.5 us (39%)
  starting transfers between devices  26.5 us (29%)
  blocking collectives  16.9 us (19%)
  Pallas kernels  9.77 us (11%)
  local copies, waits for them, and re-layouts  0.96 us (1%)
    all_to_all x1, blocking collectives, per_device(): lax.all_to_all(terms, 'near', split_axis=0, concat_axis=0, tiled=True)  16.9 us
    all_to_all x1, starting transfers between devices, per_device(): lax.all_to_all(pieces, everyone, split_axis=0, concat_axis=0, tiled=True)  15.7 us
    all_to_all x1, waiting for transfers between devices, per_device(): lax.all_to_all(pieces, everyone, split_axis=0, concat_axis=0, tiled=True)  15.3 us
    all_to_all x1, waiting for transfers between devices, per_device(): lax.all_to_all(summed, everyone, split_axis=0, concat_axis=0, tiled=True)  12.4 us
    all_to_all x1, waiting for transfers between devices, per_device(): lax.all_to_all(picked, 'near', split_axis=0, concat_axis=0, tiled=True)  7.82 us
    all_to_all x1, starting transfers between devices, per_device(): lax.all_to_all(summed, everyone, split_axis=0, concat_axis=0, tiled=True)  7.3 us
    all_to_all x1, starting transfers between devices, per_device(): lax.all_to_all(picked, 'near', split_axis=0, concat_axis=0, tiled=True)  3.51 us
    pallas_call x1, Pallas kernels, per_device(): pl.pallas_call(late_kernel, out_shape=(shaped((BLK, GROUP * HD), low), sh...  2.09 us
  transfers between devices with their start and end apart: 3, of which 3 were waited for; matrix products, arithmetic and copies ran while one was open for 0% of the time, Pallas kernels for 2%

profile of v1, /device:TPU:1, one launch (start us, length us, event | category | flops | bytes accessed | tf_op | source)
XLA Modules:
  0.0 90.3 jit_solution(6912980803649618208)
XLA Ops:
  0.6 0.0 copy-start.1
  0.6 0.0 copy-start
  0.7 1.6 %cut.1 = bf16[1024,128]{1,0:T(8,128)(2,1)} custom-call(bf16[16,1024]{1,0:T(8,128)(2,1)} %key_hbm.1, bf16[16,1024]{1,0:T(8,128)(2,1)} %value_hbm.1), custom_call_target="tpu_custom_call" | custom-call | tf_op jit(solution)/shard_map/cut/pallas_call | solution.py:271
  2.2 15.7 %all-to-all-start = ((bf16[256,4,128]{2,1,0:T(4,128)(2,1)}), bf16[256,4,128]{2,1,0:T(4,128)(2,1)S(1)}, u32[]{:S(2)}, u32[]{:S(2)}) async-start(bf16[256,4,128]{2,1,0:T(4,128)(2,1)} %bitcast.2), calls=%async_computation | async-start | bytes 524288 | tf_op jit(solution)/shard_map/all_to_all | solution.py:284
  17.9 15.3 %all-to-all-done = bf16[256,4,128]{2,1,0:T(4,128)(2,1)S(1)} async-done(((bf16[256,4,128]{2,1,0:T(4,128)(2,1)}), bf16[256,4,128]{2,1,0:T(4,128)(2,1)S(1)}, u32[]{:S(2)}, u32[]{:S(2)}) %all-to-all-start) | async-done | bytes 262176 | tf_op jit(solution)/shard_map/all_to_all | solution.py:284
  33.2 1.6 %pick.1 = bf16[2048,128]{1,0:T(8,128)(2,1)} custom-call(s32[1]{0:T(128)} %bitcast.leaf_ref, s32[8,32]{1,0:T(8,128)} %bitcast.16, bf16[1024,128]{1,0:T(8,128)(2,1)S(1)} %bitcast.14), custom_call_target="tpu_custom_call" | custom-call | tf_op jit(solution)/shard_map/pick/pallas_call | solution.py:293
  34.8 3.5 %all-to-all-start.1 = ((bf16[8,256,128]{2,1,0:T(8,128)(2,1)}), bf16[8,256,128]{2,1,0:T(8,128)(2,1)S(1)}, u32[]{:S(2)}, u32[]{:S(2)}) async-start(bf16[8,256,128]{2,1,0:T(8,128)(2,1)} %bitcast.4), calls=%async_computation.1 | async-start | bytes 1048576 | tf_op jit(solution)/shard_map/all_to_all | solution.py:302
  38.3 0.0 copy-done.1
  38.3 0.0 copy-done
  38.3 0.1 prep.1.in_ref
  38.4 7.8 %all-to-all-done.1 = bf16[8,256,128]{2,1,0:T(8,128)(2,1)S(1)} async-done(((bf16[8,256,128]{2,1,0:T(8,128)(2,1)}), bf16[8,256,128]{2,1,0:T(8,128)(2,1)S(1)}, u32[]{:S(2)}, u32[]{:S(2)}) %all-to-all-start.1) | async-done | bytes 524320 | tf_op jit(solution)/shard_map/all_to_all | solution.py:302
  46.3 2.0 %attend.1 = (bf16[2048,128]{1,0:T(8,128)(2,1)S(1)}, bf16[8,128,1024]{2,1,0:T(8,128)(2,1)S(1)}, bf16[128,1024]{1,0:T(8,128)(2,1)S(1)}) custom-call(s32[1]{0:T(128)} %bitcast.leaf_ref, s32[8,32]{1,0:T(8,128)} %bitcast.17, s32[32]{0:T(128)} %len_ref.1, bf16[3072,128]{1,0:T(8,128)(2,1)S(1)} %prep.1.in_ref, bf16[2048,128]{1,0:T(8,128)(2,1)S(1)} %bitcast.10), custom_call_target="tpu_custom_call" | custom-call | tf_op jit(solution)/shard_map/attend/pallas_call | solution.py:303
  48.2 0.0 copy-start.2
  48.2 16.9 %all_to_all.44 = bf16[8,256,128]{2,1,0:T(8,128)(2,1)S(1)} all-to-all(bf16[8,256,128]{2,1,0:T(8,128)(2,1)S(1)} %bitcast.15), channel_id=1, replica_groups=mesh['far'=4,'near'=8,'head'=8] {'near'}, dimensions={0} | all-to-all | bytes 1048576 | tf_op jit(solution)/shard_map/all_to_all | solution.py:321
  65.1 1.7 %add.5 = bf16[1024,128]{1,0:T(8,128)(2,1)} custom-call(s32[1]{0:T(128)} %bitcast.leaf_ref, s32[8,32]{1,0:T(8,128)} %bitcast.18, bf16[2048,128]{1,0:T(8,128)(2,1)S(1)} %bitcast.12), custom_call_target="tpu_custom_call" | custom-call | tf_op jit(solution)/shard_map/add/pallas_call | solution.py:331
  66.9 0.0 copy-done.2
  66.9 7.3 %all-to-all-start.3 = ((bf16[256,4,128]{2,1,0:T(4,128)(2,1)}), bf16[256,4,128]{2,1,0:T(4,128)(2,1)S(1)}, u32[]{:S(2)}, u32[]{:S(2)}) async-start(bf16[256,4,128]{2,1,0:T(4,128)(2,1)} %bitcast.8), calls=%async_computation.3 | async-start | bytes 524288 | tf_op jit(solution)/shard_map/all_to_all | solution.py:343
  74.2 0.0 copy-start.3
  74.2 0.9 %copy-done.3 = bf16[128,1024]{1,0:T(8,128)(2,1)S(1)} copy-done((bf16[128,1024]{1,0:T(8,128)(2,1)S(1)}, bf16[128,1024]{1,0:T(8,128)(2,1)}, u32[]{:S(2)}) %copy-start.3) | copy-done | bytes 262168
  75.1 2.1 %late.1 = (bf16[128,1024]{1,0:T(8,128)(2,1)}, f32[128,1024]{1,0:T(8,128)}) custom-call(s32[1]{0:T(128)} %bitcast.leaf_ref, s32[8,32]{1,0:T(8,128)} %bitcast.19, bf16[2048,128]{1,0:T(8,128)(2,1)S(1)} %bitcast.11, bf16[8,128,1024]{2,1,0:T(8,128)(2,1)S(1)} %get-tuple-element.11.dl_ref, bf16[128,1024]{1,0:T(8,128)(2,1)S(1)} %copy-done.3), custom_call_target="tpu_custom_call" | custom-call | tf_op jit(solution)/shard_map/late/pallas_call | solution.py:322
  77.2 12.4 %all-to-all-done.3 = bf16[256,4,128]{2,1,0:T(4,128)(2,1)S(1)} async-done(((bf16[256,4,128]{2,1,0:T(4,128)(2,1)}), bf16[256,4,128]{2,1,0:T(4,128)(2,1)S(1)}, u32[]{:S(2)}, u32[]{:S(2)}) %all-to-all-start.3) | async-done | bytes 262176 | tf_op jit(solution)/shard_map/all_to_all | solution.py:343
  89.6 0.7 finish.1
Async XLA Ops:
  0.6 37.6 %copy-start.1 = (bf16[128,1024]{1,0:T(8,128)(2,1)S(1)}, bf16[128,1024]{1,0:T(8,128)(2,1)}, u32[]{:S(2)}) copy-start(bf16[128,1024]{1,0:T(8,128)(2,1)} %g_ref.1) | copy-start | bytes 786436
  0.6 37.6 %copy-start = (bf16[128,1024]{1,0:T(8,128)(2,1)S(1)}, bf16[128,1024]{1,0:T(8,128)(2,1)}, u32[]{:S(2)}) copy-start(bf16[128,1024]{1,0:T(8,128)(2,1)} %q_ref.1) | copy-start | bytes 786436
  2.2 30.9 %all-to-all-start = ((bf16[256,4,128]{2,1,0:T(4,128)(2,1)}), bf16[256,4,128]{2,1,0:T(4,128)(2,1)S(1)}, u32[]{:S(2)}, u32[]{:S(2)}) async-start(bf16[256,4,128]{2,1,0:T(4,128)(2,1)} %bitcast.2), calls=%async_computation | async-start | bytes 524288 | tf_op jit(solution)/shard_map/all_to_all | solution.py:284
  34.8 11.5 %all-to-all-start.1 = ((bf16[8,256,128]{2,1,0:T(8,128)(2,1)}), bf16[8,256,128]{2,1,0:T(8,128)(2,1)S(1)}, u32[]{:S(2)}, u32[]{:S(2)}) async-start(bf16[8,256,128]{2,1,0:T(8,128)(2,1)} %bitcast.4), calls=%async_computation.1 | async-start | bytes 1048576 | tf_op jit(solution)/shard_map/all_to_all | solution.py:302
  48.2 18.6 %copy-start.2 = (bf16[128,1024]{1,0:T(8,128)(2,1)}, bf16[128,1024]{1,0:T(8,128)(2,1)S(1)}, u32[]{:S(2)}) copy-start(bf16[128,1024]{1,0:T(8,128)(2,1)S(1)} %get-tuple-element.12.out_t_ref) | copy-start | bytes 786436
  66.9 22.7 %all-to-all-start.3 = ((bf16[256,4,128]{2,1,0:T(4,128)(2,1)}), bf16[256,4,128]{2,1,0:T(4,128)(2,1)S(1)}, u32[]{:S(2)}, u32[]{:S(2)}) async-start(bf16[256,4,128]{2,1,0:T(4,128)(2,1)} %bitcast.8), calls=%async_computation.3 | async-start | bytes 524288 | tf_op jit(solution)/shard_map/all_to_all | solution.py:343
  74.2 1.0 %copy-start.3 = (bf16[128,1024]{1,0:T(8,128)(2,1)S(1)}, bf16[128,1024]{1,0:T(8,128)(2,1)}, u32[]{:S(2)}) copy-start(bf16[128,1024]{1,0:T(8,128)(2,1)} %copy-done.2) | copy-start | bytes 786436

commit v2 on v1

--- a/solution.py
+++ b/solution.py
@@ -47,6 +47,14 @@
                 out_ref[first : first + SHARE, :] = share
 
 
+def table_kernel(leaf_ref, anc_ref, len_ref, out_ref):
+    for n in range(NODES):
+        for a in range(ANC):
+            out_ref[a, n] = anc_ref[a, n]
+        out_ref[ANC, n] = len_ref[n]
+    out_ref[ANC + 1, 0] = leaf_ref[0]
+
+
 def prep_kernel(q_ref, g_ref, out_ref):
     for h in range(GROUP):
         here = slice(h * HD, (h + 1) * HD)
@@ -56,8 +64,8 @@
             out_ref[first : first + BLK, :] = block
 
 
-def levels_of(leaf_ref, anc_ref):
-    base = (leaf_ref[0] // NEAR) * NEAR
+def levels_of(anc_ref):
+    base = (anc_ref[ANC + 1, 0] // NEAR) * NEAR
     for s in range(ANC):
         nodes = [anc_ref[s, base + j] for j in range(NEAR)]
         highest = nodes[0]
@@ -66,8 +74,8 @@
         yield s, nodes, highest >= 0
 
 
-def pick_kernel(leaf_ref, anc_ref, rows_ref, out_ref, sems):
-    levels = list(levels_of(leaf_ref, anc_ref))
+def pick_kernel(anc_ref, rows_ref, out_ref, sems):
+    levels = list(levels_of(anc_ref))
     for s, nodes, some in levels:
 
         @pl.when(some)
@@ -85,7 +93,7 @@
             pltpu.make_async_copy(block, block, sems.at[s]).wait()
 
 
-def add_kernel(leaf_ref, anc_ref, terms_ref, out_ref, even_ref, odd_ref):
+def add_kernel(anc_ref, terms_ref, out_ref, even_ref, odd_ref):
     def term(j, s):
         first = (j * ANC + s) * SHARE
         return terms_ref[first : first + SHARE, :].astype(jnp.float32)
@@ -96,7 +104,7 @@
     even_ref[:SHARE, :] = root
     even_ref[SHARE:, :] = jnp.zeros_like(even_ref[SHARE:, :])
     odd_ref[...] = jnp.zeros_like(odd_ref)
-    for s, nodes, some in levels_of(leaf_ref, anc_ref):
+    for s, nodes, some in levels_of(anc_ref):
         if s == 0:
             continue
 
@@ -142,10 +150,10 @@
 
 
 def attention_kernel(
-    leaf_ref, anc_ref, len_ref, in_ref, kv_ref, kvg_ref, dl_ref, out_ref,
+    anc_ref, in_ref, kv_ref, kvg_ref, dl_ref, out_ref,
     e_ref, top_ref, sum_ref, acc_ref,
 ):
-    leaf = leaf_ref[0]
+    leaf = anc_ref[ANC + 1, 0]
     used = used_slots(anc_ref, leaf)
 
     def stacked(part, strip):
@@ -165,7 +173,7 @@
 
     def logits_pass(s, carry):
         node = anc_ref[s, leaf]
-        length = len_ref[node]
+        length = anc_ref[ANC, node]
         ends = jnp.where(node == leaf, jnp.minimum(query + 1, length), length)
         seen = jnp.concatenate([place < ends] * (STRIP // BLK), axis=1)
         key = keys_of(kv_ref, s, 0)
@@ -218,8 +226,8 @@
 
     lax.fori_loop(0, used, gradient_pass, 0)
 
-def late_kernel(leaf_ref, anc_ref, kv_ref, dl_ref, out_t_ref, out_ref, qg_ref, acc_ref):
-    used = used_slots(anc_ref, leaf_ref[0])
+def late_kernel(anc_ref, kv_ref, dl_ref, out_t_ref, out_ref, qg_ref, acc_ref):
+    used = used_slots(anc_ref, anc_ref[ANC + 1, 0])
     for h in range(GROUP):
         here = slice(h * BLK, (h + 1) * BLK)
         out_ref[:, here] = out_t_ref[:, here].T
@@ -270,7 +278,7 @@
     low, wide = jnp.bfloat16, jnp.float32
     pieces = pl.pallas_call(
         cut_kernel,
-        out_shape=shaped((FAR * NEAR * SHARE, HD), low),
+        out_shape=pltpu.VMEM((FAR * NEAR * SHARE, HD), low),
         in_specs=[HBM, HBM],
         out_specs=VMEM,
         scratch_shapes=[
@@ -281,6 +289,14 @@
         compiler_params=room(4),
         name="cut",
     )(far_memory(key_in), far_memory(value_in))
+    table = pl.pallas_call(
+        table_kernel,
+        out_shape=pltpu.SMEM((2 * ANC, NODES), jnp.int32),
+        in_specs=[SMEM, SMEM, SMEM],
+        out_specs=SMEM,
+        compiler_params=room(1),
+        name="table",
+    )(leaf, ancestry_t, node_len)
     shares = lax.all_to_all(pieces, everyone, split_axis=0, concat_axis=0, tiled=True)
     stacked = pl.pallas_call(
         prep_kernel,
@@ -290,24 +306,26 @@
         compiler_params=room(4),
         name="prep",
     )(query_in, out_grad)
+    shares, stacked, table = lax.optimization_barrier((shares, stacked, table))
+    table = pltpu.with_memory_space_constraint(table, pltpu.SMEM)
     picked = pl.pallas_call(
         pick_kernel,
-        out_shape=shaped((NEAR * ANC * SHARE, HD), low),
-        in_specs=[SMEM, SMEM, VMEM],
-        out_specs=ANY,
+        out_shape=pltpu.VMEM((NEAR * ANC * SHARE, HD), low),
+        in_specs=[SMEM, VMEM],
+        out_specs=VMEM,
         scratch_shapes=[pltpu.SemaphoreType.DMA((ANC,))],
         compiler_params=room(4),
         name="pick",
-    )(leaf, ancestry_t, near_memory(shares))
+    )(table, near_memory(shares))
     kv = near_memory(lax.all_to_all(picked, "near", split_axis=0, concat_axis=0, tiled=True))
     terms, dlogit, out_t = pl.pallas_call(
         attention_kernel,
         out_shape=(
-            shaped((2 * ANC * BLK, HD), low),
+            pltpu.VMEM((2 * ANC * BLK, HD), low),
             pltpu.VMEM((ANC, BLK, WIDE), low),
             pltpu.VMEM((HD, WIDE), low),
         ),
-        in_specs=[SMEM, SMEM, SMEM, VMEM, VMEM],
+        in_specs=[SMEM, VMEM, VMEM],
         out_specs=(VMEM, VMEM, VMEM),
         scratch_shapes=[
             pltpu.VMEM((ANC, BLK, WIDE), wide),
@@ -317,21 +335,21 @@
         ],
         compiler_params=room(16),
         name="attend",
-    )(leaf, ancestry_t, node_len, near_memory(stacked), kv)
+    )(table, near_memory(stacked), kv)
     terms = lax.all_to_all(terms, "near", split_axis=0, concat_axis=0, tiled=True)
     attended, query_grad = pl.pallas_call(
         late_kernel,
         out_shape=(shaped((BLK, GROUP * HD), low), shaped((BLK, GROUP * HD), wide)),
-        in_specs=[SMEM, SMEM, VMEM, VMEM, VMEM],
+        in_specs=[SMEM, VMEM, VMEM, VMEM],
         out_specs=(VMEM, VMEM),
         scratch_shapes=[pltpu.VMEM((HD, WIDE), wide)],
         compiler_params=room(8),
         name="late",
-    )(leaf, ancestry_t, kv, near_memory(dlogit), near_memory(out_t))
+    )(table, kv, near_memory(dlogit), near_memory(out_t))
     summed = pl.pallas_call(
         add_kernel,
-        out_shape=shaped((NODES * SHARE, HD), low),
-        in_specs=[SMEM, SMEM, VMEM],
+        out_shape=pltpu.VMEM((NODES * SHARE, HD), low),
+        in_specs=[SMEM, VMEM],
         out_specs=VMEM,
         scratch_shapes=[
             pltpu.VMEM(((NODES + 1) * SHARE, HD), wide),
@@ -339,7 +357,7 @@
         ],
         compiler_params=room(8),
         name="add",
-    )(leaf, ancestry_t, near_memory(terms))
+    )(table, near_memory(terms))
     back = lax.all_to_all(summed, everyone, split_axis=0, concat_axis=0, tiled=True)
     key_grad, value_grad = pl.pallas_call(
         finish_kernel,

time: 90.7 us -> 86.2 us (0.950)
  waiting for transfers between devices: 35.5 us -> 25.2 us
  blocking collectives: 16.9 us -> 23.3 us
  Pallas kernels: 9.77 us -> 7.76 us
  local copies, waits for them, and re-layouts: 0.96 us -> 2.85 us
  starting transfers between devices: 26.5 us -> 25.3 us
    all_to_all x0 -> x1, blocking collectives: none -> 10.3 us  [per_device(): lax.all_to_all(picked, 'near', split_axis=0, concat_axis=0, tiled=True)]
    all_to_all x1 -> x0, waiting for transfers between devices: 7.82 us -> none  [per_device(): lax.all_to_all(picked, 'near', split_axis=0, concat_axis=0, tiled=True)]
    all_to_all x1, blocking collectives: 16.9 us -> 13 us  [per_device(): lax.all_to_all(terms, 'near', split_axis=0, concat_axis=0, tiled=True)]
    all_to_all x1 -> x0, starting transfers between devices: 3.51 us -> none  [per_device(): lax.all_to_all(picked, 'near', split_axis=0, concat_axis=0, tiled=True)]
    all_to_all x1, waiting for transfers between devices: 15.3 us -> 12.3 us  [per_device(): lax.all_to_all(pieces, everyone, split_axis=0, concat_axis=0, tiled=True)]
    all_to_all x1, starting transfers between devices: 7.3 us -> 9.65 us  [per_device(): lax.all_to_all(summed, everyone, split_axis=0, concat_axis=0, tiled=True)]
    unnamed x8, local copies, waits for them, and re-layouts: 0.96 us -> 2.85 us
    pallas_call x4 -> x5, Pallas kernels: 6.86 us -> 5.57 us  [the longest x1 1.51 us: per_device(): pl.pallas_call(cut_kernel, out_shape=pltpu.VMEM((FAR * NEAR * SHARE, HD),...]
  transfers between devices with their start and end apart: 3 -> 2, of which waited for: 3 -> 2; matrix products, arithmetic and copies ran while one was open for 0% -> 0% of each run, Pallas kernels for 2% -> 3%
where the time goes in v2:
time: 86.2 us; the launch traced here: 85.1 us
  starting transfers between devices  25.3 us (29%)
  waiting for transfers between devices  25.2 us (29%)
  blocking collectives  23.3 us (27%)
  Pallas kernels  7.76 us (9%)
  local copies, waits for them, and re-layouts  2.85 us (3%)
    all_to_all x1, starting transfers between devices, per_device(): lax.all_to_all(pieces, everyone, split_axis=0, concat_axis=0, tiled=True)  15.7 us
    all_to_all x1, blocking collectives, per_device(): lax.all_to_all(terms, 'near', split_axis=0, concat_axis=0, tiled=True)  13 us
    all_to_all x1, waiting for transfers between devices, per_device(): lax.all_to_all(summed, everyone, split_axis=0, concat_axis=0, tiled=True)  13 us
    all_to_all x1, waiting for transfers between devices, per_device(): lax.all_to_all(pieces, everyone, split_axis=0, concat_axis=0, tiled=True)  12.3 us
    all_to_all x1, blocking collectives, per_device(): lax.all_to_all(picked, 'near', split_axis=0, concat_axis=0, tiled=True)  10.3 us
    all_to_all x1, starting transfers between devices, per_device(): lax.all_to_all(summed, everyone, split_axis=0, concat_axis=0, tiled=True)  9.65 us
    unnamed x8, local copies, waits for them, and re-layouts  2.85 us
  transfers between devices with their start and end apart: 2, of which 2 were waited for; matrix products, arithmetic and copies ran while one was open for 0% of the time, Pallas kernels for 3%

profile of v2, /device:TPU:1, one launch (start us, length us, event | category | flops | bytes accessed | tf_op | source)
XLA Modules:
  0.0 85.1 jit_solution(12065790231923468555)
XLA Ops:
  0.6 1.5 %cut.1 = bf16[1024,128]{1,0:T(8,128)(2,1)} custom-call(bf16[16,1024]{1,0:T(8,128)(2,1)} %key_hbm.1, bf16[16,1024]{1,0:T(8,128)(2,1)} %value_hbm.1), custom_call_target="tpu_custom_call" | custom-call | tf_op jit(solution)/shard_map/cut/pallas_call | solution.py:279
  2.1 15.7 %all-to-all-start = ((bf16[256,4,128]{2,1,0:T(4,128)(2,1)}), bf16[256,4,128]{2,1,0:T(4,128)(2,1)S(1)}, u32[]{:S(2)}, u32[]{:S(2)}) async-start(bf16[256,4,128]{2,1,0:T(4,128)(2,1)} %bitcast), calls=%async_computation | async-start | bytes 524288 | tf_op jit(solution)/shard_map/all_to_all | solution.py:300
  17.8 0.0 copy-start
  17.8 0.9 %copy-done = bf16[128,1024]{1,0:T(8,128)(2,1)S(1)} copy-done((bf16[128,1024]{1,0:T(8,128)(2,1)S(1)}, bf16[128,1024]{1,0:T(8,128)(2,1)}, u32[]{:S(2)}) %copy-start) | copy-done | bytes 262168
  18.8 0.0 copy-start.1
  18.8 0.9 %copy-done.1 = bf16[128,1024]{1,0:T(8,128)(2,1)S(1)} copy-done((bf16[128,1024]{1,0:T(8,128)(2,1)S(1)}, bf16[128,1024]{1,0:T(8,128)(2,1)}, u32[]{:S(2)}) %copy-start.1) | copy-done | bytes 262168
  19.7 0.1 prep.1.in_ref
  19.9 1.0 %table.1.anc_ref = s32[16,32]{1,0:T(8,128)S(4)} custom-call(s32[1]{0:T(128)} %bitcast.2.leaf_ref, s32[8,32]{1,0:T(8,128)} %bitcast.17, s32[32]{0:T(128)} %len_ref.1), custom_call_target="tpu_custom_call" | custom-call | tf_op jit(solution)/shard_map/table/pallas_call | solution.py:292
  20.8 12.3 %all-to-all-done = bf16[256,4,128]{2,1,0:T(4,128)(2,1)S(1)} async-done(((bf16[256,4,128]{2,1,0:T(4,128)(2,1)}), bf16[256,4,128]{2,1,0:T(4,128)(2,1)S(1)}, u32[]{:S(2)}, u32[]{:S(2)}) %all-to-all-start) | async-done | bytes 262176 | tf_op jit(solution)/shard_map/all_to_all | solution.py:300
  33.1 0.8 pick.1
  33.9 10.3 %all_to_all.45 = bf16[8,256,128]{2,1,0:T(8,128)(2,1)S(1)} all-to-all(bf16[8,256,128]{2,1,0:T(8,128)(2,1)S(1)} %bitcast.12), channel_id=1, replica_groups=mesh['far'=4,'near'=8,'head'=8] {'near'}, dimensions={0} | all-to-all | bytes 1048576 | tf_op jit(solution)/shard_map/all_to_all | solution.py:320
  44.2 1.2 %attend.1 = (bf16[2048,128]{1,0:T(8,128)(2,1)S(1)}, bf16[8,128,1024]{2,1,0:T(8,128)(2,1)S(1)}, bf16[128,1024]{1,0:T(8,128)(2,1)S(1)}) custom-call(s32[16,32]{1,0:T(8,128)S(4)} %table.1.anc_ref, bf16[3072,128]{1,0:T(8,128)(2,1)S(1)} %prep.1.in_ref, bf16[2048,128]{1,0:T(8,128)(2,1)S(1)} %bitcast.10), custom_call_target="tpu_custom_call" | custom-call | tf_op jit(solution)/shard_map/attend/pallas_call | solution.py:321
  45.4 0.0 copy-start.2
  45.4 13.0 %all_to_all.46 = bf16[8,256,128]{2,1,0:T(8,128)(2,1)S(1)} all-to-all(bf16[8,256,128]{2,1,0:T(8,128)(2,1)S(1)} %bitcast.16), channel_id=1, replica_groups=mesh['far'=4,'near'=8,'head'=8] {'near'}, dimensions={0} | all-to-all | bytes 1048576 | tf_op jit(solution)/shard_map/all_to_all | solution.py:339
  58.4 1.0 %add.5 = bf16[1024,128]{1,0:T(8,128)(2,1)} custom-call(s32[16,32]{1,0:T(8,128)S(4)} %table.1.anc_ref, bf16[2048,128]{1,0:T(8,128)(2,1)S(1)} %bitcast.13), custom_call_target="tpu_custom_call" | custom-call | tf_op jit(solution)/shard_map/add/pallas_call | solution.py:349
  59.5 0.0 copy-done.2
  59.5 9.6 %all-to-all-start.3 = ((bf16[256,4,128]{2,1,0:T(4,128)(2,1)}), bf16[256,4,128]{2,1,0:T(4,128)(2,1)S(1)}, u32[]{:S(2)}, u32[]{:S(2)}) async-start(bf16[256,4,128]{2,1,0:T(4,128)(2,1)} %bitcast.8), calls=%async_computation.3 | async-start | bytes 524288 | tf_op jit(solution)/shard_map/all_to_all | solution.py:361
  69.1 0.0 copy-start.3
  69.1 0.9 %copy-done.3 = bf16[128,1024]{1,0:T(8,128)(2,1)S(1)} copy-done((bf16[128,1024]{1,0:T(8,128)(2,1)S(1)}, bf16[128,1024]{1,0:T(8,128)(2,1)}, u32[]{:S(2)}) %copy-start.3) | copy-done | bytes 262168
  70.1 1.4 %late.1 = (bf16[128,1024]{1,0:T(8,128)(2,1)}, f32[128,1024]{1,0:T(8,128)}) custom-call(s32[16,32]{1,0:T(8,128)S(4)} %table.1.anc_ref, bf16[2048,128]{1,0:T(8,128)(2,1)S(1)} %bitcast.11, bf16[8,128,1024]{2,1,0:T(8,128)(2,1)S(1)} %get-tuple-element.17.dl_ref, bf16[128,1024]{1,0:T(8,128)(2,1)S(1)} %copy-done.3), custom_call_target="tpu_custom_call" | custom-call | tf_op jit(solution)/shard_map/late/pallas_call | solution.py:340
  71.5 13.0 %all-to-all-done.3 = bf16[256,4,128]{2,1,0:T(4,128)(2,1)S(1)} async-done(((bf16[256,4,128]{2,1,0:T(4,128)(2,1)}), bf16[256,4,128]{2,1,0:T(4,128)(2,1)S(1)}, u32[]{:S(2)}, u32[]{:S(2)}) %all-to-all-start.3) | async-done | bytes 262176 | tf_op jit(solution)/shard_map/all_to_all | solution.py:361
  84.4 0.7 finish.1
Async XLA Ops:
  2.1 30.9 %all-to-all-start = ((bf16[256,4,128]{2,1,0:T(4,128)(2,1)}), bf16[256,4,128]{2,1,0:T(4,128)(2,1)S(1)}, u32[]{:S(2)}, u32[]{:S(2)}) async-start(bf16[256,4,128]{2,1,0:T(4,128)(2,1)} %bitcast), calls=%async_computation | async-start | bytes 524288 | tf_op jit(solution)/shard_map/all_to_all | solution.py:300
  17.8 1.0 %copy-start = (bf16[128,1024]{1,0:T(8,128)(2,1)S(1)}, bf16[128,1024]{1,0:T(8,128)(2,1)}, u32[]{:S(2)}) copy-start(bf16[128,1024]{1,0:T(8,128)(2,1)} %q_ref.1) | copy-start | bytes 786436
  18.8 0.9 %copy-start.1 = (bf16[128,1024]{1,0:T(8,128)(2,1)S(1)}, bf16[128,1024]{1,0:T(8,128)(2,1)}, u32[]{:S(2)}) copy-start(bf16[128,1024]{1,0:T(8,128)(2,1)} %g_ref.1) | copy-start | bytes 786436
  45.4 14.0 %copy-start.2 = (bf16[128,1024]{1,0:T(8,128)(2,1)}, bf16[128,1024]{1,0:T(8,128)(2,1)S(1)}, u32[]{:S(2)}) copy-start(bf16[128,1024]{1,0:T(8,128)(2,1)S(1)} %get-tuple-element.18.out_t_ref) | copy-start | bytes 786436
  59.5 25.0 %all-to-all-start.3 = ((bf16[256,4,128]{2,1,0:T(4,128)(2,1)}), bf16[256,4,128]{2,1,0:T(4,128)(2,1)S(1)}, u32[]{:S(2)}, u32[]{:S(2)}) async-start(bf16[256,4,128]{2,1,0:T(4,128)(2,1)} %bitcast.8), calls=%async_computation.3 | async-start | bytes 524288 | tf_op jit(solution)/shard_map/all_to_all | solution.py:361
  69.1 1.0 %copy-start.3 = (bf16[128,1024]{1,0:T(8,128)(2,1)S(1)}, bf16[128,1024]{1,0:T(8,128)(2,1)}, u32[]{:S(2)}) copy-start(bf16[128,1024]{1,0:T(8,128)(2,1)} %copy-done.2) | copy-start | bytes 786436

commit v3 on v2

--- a/solution.py
+++ b/solution.py
@@ -134,9 +134,26 @@
             ref[:, h * HD : (h + 1) * HD] = jnp.concatenate(rows, axis=0)
 
 
-def keys_of(kv_ref, s, kind):
+def keys_of(kv_ref, s, slots, kind):
+    wide = slots * SHARE
     firsts = [((2 * quad + kind) * ANC + s) * SHARE for quad in range(QUADS)]
-    return jnp.concatenate([kv_ref[pl.ds(pl.multiple_of(f, SHARE), SHARE), :] for f in firsts], axis=0)
+    return jnp.concatenate([kv_ref[pl.ds(pl.multiple_of(f, wide), wide), :] for f in firsts], axis=0)
+
+
+def rows_of(s, slots):
+    return pl.ds(pl.multiple_of(s * BLK, slots * BLK), slots * BLK)
+
+
+def over_slots(used, turn):
+    def both(pair, carry):
+        turn(2 * pair, 2)
+        return carry
+
+    lax.fori_loop(0, used // 2, both, 0)
+
+    @pl.when(used % 2 == 1)
+    def _():
+        turn(used - 1, 1)
 
 
 def used_slots(anc_ref, leaf):
@@ -151,7 +168,7 @@
 
 def attention_kernel(
     anc_ref, in_ref, kv_ref, kvg_ref, dl_ref, out_ref,
-    e_ref, top_ref, sum_ref, acc_ref,
+    e_ref, p_ref, top_ref, sum_ref, acc_ref,
 ):
     leaf = anc_ref[ANC + 1, 0]
     used = used_slots(anc_ref, leaf)
@@ -167,64 +184,66 @@
     sum_ref[...] = jnp.zeros_like(sum_ref)
     acc_ref[...] = jnp.zeros_like(acc_ref)
 
-    row = lax.broadcasted_iota(jnp.int32, (BLK, BLK), 0)
-    place = ((row // PIECE) % KVH) * 16 + (row // SHARE) * PIECE + row % PIECE
-    query = lax.broadcasted_iota(jnp.int32, (BLK, BLK), 1)
-
-    def logits_pass(s, carry):
+    def ends_of(s, query):
         node = anc_ref[s, leaf]
         length = anc_ref[ANC, node]
-        ends = jnp.where(node == leaf, jnp.minimum(query + 1, length), length)
+        return jnp.where(node == leaf, jnp.minimum(query + 1, length), length)
+
+    def logits_turn(s, slots):
+        shape = (slots * BLK, BLK)
+        row = lax.broadcasted_iota(jnp.int32, shape, 0)
+        query = lax.broadcasted_iota(jnp.int32, shape, 1)
+        place = ((row // PIECE) % KVH) * 16 + (row // (slots * SHARE)) * PIECE + row % PIECE
+        ends = ends_of(s, query)
+        if slots == 2:
+            ends = jnp.where((row // SHARE) % 2 == 1, ends_of(s + 1, query), ends)
         seen = jnp.concatenate([place < ends] * (STRIP // BLK), axis=1)
-        key = keys_of(kv_ref, s, 0)
+        key = keys_of(kv_ref, s, slots, 0)
         for strip in STRIPS:
             raw = dot(key, stacked(0, strip), NT) * (SCALE * LOG2E)
             raw = jnp.where(seen, raw, LOW)
-            e_ref[s, :, strip] = raw
-            high = jnp.max(raw.reshape(BLK // 8, 8, STRIP), axis=0)
+            e_ref[rows_of(s, slots), strip] = raw
+            high = jnp.max(raw.reshape(slots * BLK // 8, 8, STRIP), axis=0)
             top_ref[:, strip] = jnp.maximum(top_ref[:, strip], high)
-        return carry
-
-    lax.fori_loop(0, used, logits_pass, 0)
+
+    over_slots(used, logits_turn)
     top_ref[...] = jnp.broadcast_to(jnp.max(top_ref[...], axis=0, keepdims=True), top_ref.shape)
 
-    def output_pass(s, carry):
-        value_t = keys_of(kv_ref, s, 1).T
+    def output_turn(s, slots):
+        value_t = keys_of(kv_ref, s, slots, 1).T
         for strip in STRIPS:
-            expo = jnp.exp2(e_ref[s, :, strip] - top_ref[:1, strip])
-            e_ref[s, :, strip] = expo
-            sum_ref[:, strip] = sum_ref[:, strip] + jnp.sum(expo.reshape(BLK // 8, 8, STRIP), axis=0)
+            expo = jnp.exp2(e_ref[rows_of(s, slots), strip] - top_ref[:1, strip])
+            part = jnp.sum(expo.reshape(slots * BLK // 8, 8, STRIP), axis=0)
+            sum_ref[:, strip] = sum_ref[:, strip] + part
             acc_ref[:, strip] = acc_ref[:, strip] + dot(value_t, expo.astype(jnp.bfloat16))
-        return carry
-
-    lax.fori_loop(0, used, output_pass, 0)
+
+    over_slots(used, output_turn)
     for strip in STRIPS:
-        inverse = 1.0 / jnp.sum(sum_ref[:, strip], axis=0, keepdims=True)
-        out_t = (acc_ref[:, strip] * inverse).astype(jnp.bfloat16)
+        total = jnp.sum(sum_ref[:, strip], axis=0, keepdims=True)
+        out_t = (acc_ref[:, strip] * (1.0 / total)).astype(jnp.bfloat16)
         delta = jnp.sum(turned(strip).astype(jnp.float32) * out_t.astype(jnp.float32), axis=0, keepdims=True)
-        top_ref[:1, strip] = inverse
+        top_ref[:1, strip] = top_ref[:1, strip] + jnp.log2(total)
         sum_ref[:1, strip] = delta
         out_ref[:, strip] = out_t
 
-    def gradient_pass(s, carry):
-        value = keys_of(kv_ref, s, 1)
-        key_sum = jnp.zeros((BLK, HD), jnp.float32)
-        value_sum = jnp.zeros((BLK, HD), jnp.float32)
+    def gradient_turn(s, slots):
+        value = keys_of(kv_ref, s, slots, 1)
         for strip in STRIPS:
             dprob = dot(value, turned(strip))
-            weights = e_ref[s, :, strip] * top_ref[:1, strip]
-            dlogit = (weights * (dprob - sum_ref[:1, strip])).astype(jnp.bfloat16)
-            value_sum = value_sum + dot(weights.astype(jnp.bfloat16), stacked(1, strip))
-            key_sum = key_sum + dot(dlogit, stacked(0, strip))
-            dl_ref[s, :, strip] = dlogit
-        for kind, total in ((0, key_sum * SCALE), (1, value_sum)):
+            weights = jnp.exp2(e_ref[rows_of(s, slots), strip] - top_ref[:1, strip])
+            dl_ref[rows_of(s, slots), strip] = (weights * (dprob - sum_ref[:1, strip])).astype(jnp.bfloat16)
+            p_ref[: slots * BLK, strip] = weights.astype(jnp.bfloat16)
+        key_sum = dot(dl_ref[rows_of(s, slots), :], in_ref[:WIDE, :]) * SCALE
+        value_sum = dot(p_ref[: slots * BLK, :], in_ref[WIDE : 2 * WIDE, :])
+        wide = slots * SHARE
+        for kind, total in ((0, key_sum), (1, value_sum)):
             total = total.astype(jnp.bfloat16)
             for quad in range(QUADS):
-                first = pl.multiple_of(((2 * quad + kind) * ANC + s) * SHARE, SHARE)
-                kvg_ref[pl.ds(first, SHARE), :] = total[quad * SHARE : (quad + 1) * SHARE]
-        return carry
-
-    lax.fori_loop(0, used, gradient_pass, 0)
+                first = pl.multiple_of(((2 * quad + kind) * ANC + s) * SHARE, wide)
+                kvg_ref[pl.ds(first, wide), :] = total[quad * wide : (quad + 1) * wide]
+
+    over_slots(used, gradient_turn)
+
 
 def late_kernel(anc_ref, kv_ref, dl_ref, out_t_ref, out_ref, qg_ref, acc_ref):
     used = used_slots(anc_ref, anc_ref[ANC + 1, 0])
@@ -233,13 +252,12 @@
         out_ref[:, here] = out_t_ref[:, here].T
     acc_ref[...] = jnp.zeros_like(acc_ref)
 
-    def query_pass(s, carry):
-        key_t = keys_of(kv_ref, s, 0).T
+    def query_turn(s, slots):
+        key_t = keys_of(kv_ref, s, slots, 0).T
         for strip in STRIPS:
-            acc_ref[:, strip] = acc_ref[:, strip] + dot(key_t, dl_ref[s, :, strip])
-        return carry
-
-    lax.fori_loop(0, used, query_pass, 0)
+            acc_ref[:, strip] = acc_ref[:, strip] + dot(key_t, dl_ref[rows_of(s, slots), strip])
+
+    over_slots(used, query_turn)
     for h in range(GROUP):
         here = slice(h * BLK, (h + 1) * BLK)
         qg_ref[:, here] = (acc_ref[:, here] * SCALE).T
@@ -322,13 +340,14 @@
         attention_kernel,
         out_shape=(
             pltpu.VMEM((2 * ANC * BLK, HD), low),
-            pltpu.VMEM((ANC, BLK, WIDE), low),
+            pltpu.VMEM((ANC * BLK, WIDE), low),
             pltpu.VMEM((HD, WIDE), low),
         ),
         in_specs=[SMEM, VMEM, VMEM],
         out_specs=(VMEM, VMEM, VMEM),
         scratch_shapes=[
-            pltpu.VMEM((ANC, BLK, WIDE), wide),
+            pltpu.VMEM((ANC * BLK, WIDE), wide),
+            pltpu.VMEM((2 * BLK, WIDE), low),
             pltpu.VMEM((8, WIDE), wide),
             pltpu.VMEM((8, WIDE), wide),
             pltpu.VMEM((HD, WIDE), wide),

time: 86.2 us -> 85.3 us (0.990); the launches traced: 85.1 us -> 85.3 us
  no operation moved by 1% of the time
where the time goes in v3:
time: 85.3 us
  waiting for transfers between devices  25.2 us (30%)
  starting transfers between devices  25.1 us (29%)
  blocking collectives  23.6 us (28%)
  Pallas kernels  7.83 us (9%)
  local copies, waits for them, and re-layouts  2.85 us (3%)
    all_to_all x1, starting transfers between devices, per_device(): lax.all_to_all(pieces, everyone, split_axis=0, concat_axis=0, tiled=True)  15.7 us
    all_to_all x1, blocking collectives, per_device(): lax.all_to_all(terms, 'near', split_axis=0, concat_axis=0, tiled=True)  13.3 us
    all_to_all x1, waiting for transfers between devices, per_device(): lax.all_to_all(summed, everyone, split_axis=0, concat_axis=0, tiled=True)  13 us
    all_to_all x1, waiting for transfers between devices, per_device(): lax.all_to_all(pieces, everyone, split_axis=0, concat_axis=0, tiled=True)  12.3 us
    all_to_all x1, blocking collectives, per_device(): lax.all_to_all(picked, 'near', split_axis=0, concat_axis=0, tiled=True)  10.3 us
    all_to_all x1, starting transfers between devices, per_device(): lax.all_to_all(summed, everyone, split_axis=0, concat_axis=0, tiled=True)  9.42 us
    unnamed x8, local copies, waits for them, and re-layouts  2.85 us
  transfers between devices with their start and end apart: 2, of which 2 were waited for; matrix products, arithmetic and copies ran while one was open for 0% of the time, Pallas kernels for 3%

profile of v3, /device:TPU:1, one launch (start us, length us, event | category | flops | bytes accessed | tf_op | source)
XLA Modules:
  0.0 85.3 jit_solution(13464424952713858168)
XLA Ops:
  0.6 1.5 %cut.1 = bf16[1024,128]{1,0:T(8,128)(2,1)} custom-call(bf16[16,1024]{1,0:T(8,128)(2,1)} %key_hbm.1, bf16[16,1024]{1,0:T(8,128)(2,1)} %value_hbm.1), custom_call_target="tpu_custom_call" | custom-call | tf_op jit(solution)/shard_map/cut/pallas_call | solution.py:297
  2.1 15.7 %all-to-all-start = ((bf16[256,4,128]{2,1,0:T(4,128)(2,1)}), bf16[256,4,128]{2,1,0:T(4,128)(2,1)S(1)}, u32[]{:S(2)}, u32[]{:S(2)}) async-start(bf16[256,4,128]{2,1,0:T(4,128)(2,1)} %bitcast), calls=%async_computation | async-start | bytes 524288 | tf_op jit(solution)/shard_map/all_to_all | solution.py:318
  17.8 0.0 copy-start
  17.8 0.9 %copy-done = bf16[128,1024]{1,0:T(8,128)(2,1)S(1)} copy-done((bf16[128,1024]{1,0:T(8,128)(2,1)S(1)}, bf16[128,1024]{1,0:T(8,128)(2,1)}, u32[]{:S(2)}) %copy-start) | copy-done | bytes 262168
  18.8 0.0 copy-start.1
  18.8 0.9 %copy-done.1 = bf16[128,1024]{1,0:T(8,128)(2,1)S(1)} copy-done((bf16[128,1024]{1,0:T(8,128)(2,1)S(1)}, bf16[128,1024]{1,0:T(8,128)(2,1)}, u32[]{:S(2)}) %copy-start.1) | copy-done | bytes 262168
  19.7 0.1 prep.1.in_ref
  19.9 1.0 %table.1.anc_ref = s32[16,32]{1,0:T(8,128)S(4)} custom-call(s32[1]{0:T(128)} %bitcast.2.leaf_ref, s32[8,32]{1,0:T(8,128)} %bitcast.17, s32[32]{0:T(128)} %len_ref.1), custom_call_target="tpu_custom_call" | custom-call | tf_op jit(solution)/shard_map/table/pallas_call | solution.py:310
  20.8 12.3 %all-to-all-done = bf16[256,4,128]{2,1,0:T(4,128)(2,1)S(1)} async-done(((bf16[256,4,128]{2,1,0:T(4,128)(2,1)}), bf16[256,4,128]{2,1,0:T(4,128)(2,1)S(1)}, u32[]{:S(2)}, u32[]{:S(2)}) %all-to-all-start) | async-done | bytes 262176 | tf_op jit(solution)/shard_map/all_to_all | solution.py:318
  33.1 1.0 %pick.1 = bf16[2048,128]{1,0:T(8,128)(2,1)S(1)} custom-call(s32[16,32]{1,0:T(8,128)S(4)} %table.1.anc_ref, bf16[1024,128]{1,0:T(8,128)(2,1)S(1)} %bitcast.14), custom_call_target="tpu_custom_call" | custom-call | tf_op jit(solution)/shard_map/pick/pallas_call | solution.py:329
  34.1 10.3 %all_to_all.45 = bf16[8,256,128]{2,1,0:T(8,128)(2,1)S(1)} all-to-all(bf16[8,256,128]{2,1,0:T(8,128)(2,1)S(1)} %bitcast.12), channel_id=1, replica_groups=mesh['far'=4,'near'=8,'head'=8] {'near'}, dimensions={0} | all-to-all | bytes 1048576 | tf_op jit(solution)/shard_map/all_to_all | solution.py:338
  44.3 1.1 %attend.1 = (bf16[2048,128]{1,0:T(8,128)(2,1)S(1)}, bf16[1024,1024]{1,0:T(8,128)(2,1)S(1)}, bf16[128,1024]{1,0:T(8,128)(2,1)S(1)}) custom-call(s32[16,32]{1,0:T(8,128)S(4)} %table.1.anc_ref, bf16[3072,128]{1,0:T(8,128)(2,1)S(1)} %prep.1.in_ref, bf16[2048,128]{1,0:T(8,128)(2,1)S(1)} %bitcast.10), custom_call_target="tpu_custom_call" | custom-call | tf_op jit(solution)/shard_map/attend/pallas_call | solution.py:339
  45.5 0.0 copy-start.2
  45.5 13.3 %all_to_all.46 = bf16[8,256,128]{2,1,0:T(8,128)(2,1)S(1)} all-to-all(bf16[8,256,128]{2,1,0:T(8,128)(2,1)S(1)} %bitcast.16), channel_id=1, replica_groups=mesh['far'=4,'near'=8,'head'=8] {'near'}, dimensions={0} | all-to-all | bytes 1048576 | tf_op jit(solution)/shard_map/all_to_all | solution.py:358
  58.8 1.1 %add.5 = bf16[1024,128]{1,0:T(8,128)(2,1)} custom-call(s32[16,32]{1,0:T(8,128)S(4)} %table.1.anc_ref, bf16[2048,128]{1,0:T(8,128)(2,1)S(1)} %bitcast.13), custom_call_target="tpu_custom_call" | custom-call | tf_op jit(solution)/shard_map/add/pallas_call | solution.py:368
  59.9 0.0 copy-done.2
  59.9 9.4 %all-to-all-start.3 = ((bf16[256,4,128]{2,1,0:T(4,128)(2,1)}), bf16[256,4,128]{2,1,0:T(4,128)(2,1)S(1)}, u32[]{:S(2)}, u32[]{:S(2)}) async-start(bf16[256,4,128]{2,1,0:T(4,128)(2,1)} %bitcast.8), calls=%async_computation.3 | async-start | bytes 524288 | tf_op jit(solution)/shard_map/all_to_all | solution.py:380
  69.3 0.0 copy-start.3
  69.3 0.9 %copy-done.3 = bf16[128,1024]{1,0:T(8,128)(2,1)S(1)} copy-done((bf16[128,1024]{1,0:T(8,128)(2,1)S(1)}, bf16[128,1024]{1,0:T(8,128)(2,1)}, u32[]{:S(2)}) %copy-start.3) | copy-done | bytes 262168
  70.2 1.4 %late.1 = (bf16[128,1024]{1,0:T(8,128)(2,1)}, f32[128,1024]{1,0:T(8,128)}) custom-call(s32[16,32]{1,0:T(8,128)S(4)} %table.1.anc_ref, bf16[2048,128]{1,0:T(8,128)(2,1)S(1)} %bitcast.11, bf16[1024,1024]{1,0:T(8,128)(2,1)S(1)} %get-tuple-element.17.dl_ref, bf16[128,1024]{1,0:T(8,128)(2,1)S(1)} %copy-done.3), custom_call_target="tpu_custom_call" | custom-call | tf_op jit(solution)/shard_map/late/pallas_call | solution.py:359
  71.6 13.0 %all-to-all-done.3 = bf16[256,4,128]{2,1,0:T(4,128)(2,1)S(1)} async-done(((bf16[256,4,128]{2,1,0:T(4,128)(2,1)}), bf16[256,4,128]{2,1,0:T(4,128)(2,1)S(1)}, u32[]{:S(2)}, u32[]{:S(2)}) %all-to-all-start.3) | async-done | bytes 262176 | tf_op jit(solution)/shard_map/all_to_all | solution.py:380
  84.6 0.7 finish.1
Async XLA Ops:
  2.1 30.9 %all-to-all-start = ((bf16[256,4,128]{2,1,0:T(4,128)(2,1)}), bf16[256,4,128]{2,1,0:T(4,128)(2,1)S(1)}, u32[]{:S(2)}, u32[]{:S(2)}) async-start(bf16[256,4,128]{2,1,0:T(4,128)(2,1)} %bitcast), calls=%async_computation | async-start | bytes 524288 | tf_op jit(solution)/shard_map/all_to_all | solution.py:318
  17.8 1.0 %copy-start = (bf16[128,1024]{1,0:T(8,128)(2,1)S(1)}, bf16[128,1024]{1,0:T(8,128)(2,1)}, u32[]{:S(2)}) copy-start(bf16[128,1024]{1,0:T(8,128)(2,1)} %q_ref.1) | copy-start | bytes 786436
  18.8 0.9 %copy-start.1 = (bf16[128,1024]{1,0:T(8,128)(2,1)S(1)}, bf16[128,1024]{1,0:T(8,128)(2,1)}, u32[]{:S(2)}) copy-start(bf16[128,1024]{1,0:T(8,128)(2,1)} %g_ref.1) | copy-start | bytes 786436
  45.5 14.4 %copy-start.2 = (bf16[128,1024]{1,0:T(8,128)(2,1)}, bf16[128,1024]{1,0:T(8,128)(2,1)S(1)}, u32[]{:S(2)}) copy-start(bf16[128,1024]{1,0:T(8,128)(2,1)S(1)} %get-tuple-element.18.out_t_ref) | copy-start | bytes 786436
  59.9 24.7 %all-to-all-start.3 = ((bf16[256,4,128]{2,1,0:T(4,128)(2,1)}), bf16[256,4,128]{2,1,0:T(4,128)(2,1)S(1)}, u32[]{:S(2)}, u32[]{:S(2)}) async-start(bf16[256,4,128]{2,1,0:T(4,128)(2,1)} %bitcast.8), calls=%async_computation.3 | async-start | bytes 524288 | tf_op jit(solution)/shard_map/all_to_all | solution.py:380
  69.3 1.0 %copy-start.3 = (bf16[128,1024]{1,0:T(8,128)(2,1)S(1)}, bf16[128,1024]{1,0:T(8,128)(2,1)}, u32[]{:S(2)}) copy-start(bf16[128,1024]{1,0:T(8,128)(2,1)} %copy-done.2) | copy-start | bytes 786436

commit v4 on v3

--- a/solution.py
+++ b/solution.py
@@ -184,20 +184,25 @@
     sum_ref[...] = jnp.zeros_like(sum_ref)
     acc_ref[...] = jnp.zeros_like(acc_ref)
 
-    def ends_of(s, query):
+    block = lax.broadcasted_iota(jnp.int32, (8, BLK), 0)
+    inside = (block // PIECE) * 16 + block % PIECE
+    query = lax.broadcasted_iota(jnp.int32, (8, BLK), 1)
+
+    def room_of(s):
         node = anc_ref[s, leaf]
         length = anc_ref[ANC, node]
-        return jnp.where(node == leaf, jnp.minimum(query + 1, length), length)
+        return jnp.where(node == leaf, jnp.minimum(query + 1, length), length) - inside
 
     def logits_turn(s, slots):
-        shape = (slots * BLK, BLK)
-        row = lax.broadcasted_iota(jnp.int32, shape, 0)
-        query = lax.broadcasted_iota(jnp.int32, shape, 1)
-        place = ((row // PIECE) % KVH) * 16 + (row // (slots * SHARE)) * PIECE + row % PIECE
-        ends = ends_of(s, query)
-        if slots == 2:
-            ends = jnp.where((row // SHARE) % 2 == 1, ends_of(s + 1, query), ends)
-        seen = jnp.concatenate([place < ends] * (STRIP // BLK), axis=1)
+        ends = [room_of(s + i) for i in range(slots)]
+        left = [
+            ends[i] - (quad * PIECE + pair * 32)
+            for quad in range(QUADS)
+            for i in range(slots)
+            for pair in range(SHARE // 8)
+        ]
+        seen = jnp.concatenate(left, axis=0) > 0
+        seen = jnp.concatenate([seen] * (STRIP // BLK), axis=1)
         key = keys_of(kv_ref, s, slots, 0)
         for strip in STRIPS:
             raw = dot(key, stacked(0, strip), NT) * (SCALE * LOG2E)

time: 85.3 us -> 84.8 us (level)
  no operation moved by 1% of the time
where the time goes in v4:
time: 84.8 us; the launch traced here: 84.3 us
  waiting for transfers between devices  25.2 us (30%)
  starting transfers between devices  25.1 us (30%)
  blocking collectives  22.9 us (27%)
  Pallas kernels  7.49 us (9%)
  local copies, waits for them, and re-layouts  2.85 us (3%)
    all_to_all x1, starting transfers between devices, per_device(): lax.all_to_all(pieces, everyone, split_axis=0, concat_axis=0, tiled=True)  15.7 us
    all_to_all x1, waiting for transfers between devices, per_device(): lax.all_to_all(summed, everyone, split_axis=0, concat_axis=0, tiled=True)  13 us
    all_to_all x1, blocking collectives, per_device(): lax.all_to_all(terms, 'near', split_axis=0, concat_axis=0, tiled=True)  12.6 us
    all_to_all x1, waiting for transfers between devices, per_device(): lax.all_to_all(pieces, everyone, split_axis=0, concat_axis=0, tiled=True)  12.3 us
    all_to_all x1, blocking collectives, per_device(): lax.all_to_all(picked, 'near', split_axis=0, concat_axis=0, tiled=True)  10.3 us
    all_to_all x1, starting transfers between devices, per_device(): lax.all_to_all(summed, everyone, split_axis=0, concat_axis=0, tiled=True)  9.49 us
    unnamed x8, local copies, waits for them, and re-layouts  2.85 us
  transfers between devices with their start and end apart: 2, of which 2 were waited for; matrix products, arithmetic and copies ran while one was open for 0% of the time, Pallas kernels for 3%

profile of v4, /device:TPU:1, one launch (start us, length us, event | category | flops | bytes accessed | tf_op | source)
XLA Modules:
  0.0 84.3 jit_solution(16799404108482128864)
XLA Ops:
  0.6 1.5 %cut.1 = bf16[1024,128]{1,0:T(8,128)(2,1)} custom-call(bf16[16,1024]{1,0:T(8,128)(2,1)} %key_hbm.1, bf16[16,1024]{1,0:T(8,128)(2,1)} %value_hbm.1), custom_call_target="tpu_custom_call" | custom-call | tf_op jit(solution)/shard_map/cut/pallas_call | solution.py:302
  2.1 15.7 %all-to-all-start = ((bf16[256,4,128]{2,1,0:T(4,128)(2,1)}), bf16[256,4,128]{2,1,0:T(4,128)(2,1)S(1)}, u32[]{:S(2)}, u32[]{:S(2)}) async-start(bf16[256,4,128]{2,1,0:T(4,128)(2,1)} %bitcast), calls=%async_computation | async-start | bytes 524288 | tf_op jit(solution)/shard_map/all_to_all | solution.py:323
  17.8 0.0 copy-start
  17.8 0.9 %copy-done = bf16[128,1024]{1,0:T(8,128)(2,1)S(1)} copy-done((bf16[128,1024]{1,0:T(8,128)(2,1)S(1)}, bf16[128,1024]{1,0:T(8,128)(2,1)}, u32[]{:S(2)}) %copy-start) | copy-done | bytes 262168
  18.8 0.0 copy-start.1
  18.8 0.9 %copy-done.1 = bf16[128,1024]{1,0:T(8,128)(2,1)S(1)} copy-done((bf16[128,1024]{1,0:T(8,128)(2,1)S(1)}, bf16[128,1024]{1,0:T(8,128)(2,1)}, u32[]{:S(2)}) %copy-start.1) | copy-done | bytes 262168
  19.7 0.1 prep.1.in_ref
  19.9 1.0 %table.1.anc_ref = s32[16,32]{1,0:T(8,128)S(4)} custom-call(s32[1]{0:T(128)} %bitcast.2.leaf_ref, s32[8,32]{1,0:T(8,128)} %bitcast.17, s32[32]{0:T(128)} %len_ref.1), custom_call_target="tpu_custom_call" | custom-call | tf_op jit(solution)/shard_map/table/pallas_call | solution.py:315
  20.8 12.3 %all-to-all-done = bf16[256,4,128]{2,1,0:T(4,128)(2,1)S(1)} async-done(((bf16[256,4,128]{2,1,0:T(4,128)(2,1)}), bf16[256,4,128]{2,1,0:T(4,128)(2,1)S(1)}, u32[]{:S(2)}, u32[]{:S(2)}) %all-to-all-start) | async-done | bytes 262176 | tf_op jit(solution)/shard_map/all_to_all | solution.py:323
  33.1 0.7 pick.1
  33.8 10.3 %all_to_all.45 = bf16[8,256,128]{2,1,0:T(8,128)(2,1)S(1)} all-to-all(bf16[8,256,128]{2,1,0:T(8,128)(2,1)S(1)} %bitcast.12), channel_id=1, replica_groups=mesh['far'=4,'near'=8,'head'=8] {'near'}, dimensions={0} | all-to-all | bytes 1048576 | tf_op jit(solution)/shard_map/all_to_all | solution.py:343
  44.0 1.1 %attend.1 = (bf16[2048,128]{1,0:T(8,128)(2,1)S(1)}, bf16[1024,1024]{1,0:T(8,128)(2,1)S(1)}, bf16[128,1024]{1,0:T(8,128)(2,1)S(1)}) custom-call(s32[16,32]{1,0:T(8,128)S(4)} %table.1.anc_ref, bf16[3072,128]{1,0:T(8,128)(2,1)S(1)} %prep.1.in_ref, bf16[2048,128]{1,0:T(8,128)(2,1)S(1)} %bitcast.10), custom_call_target="tpu_custom_call" | custom-call | tf_op jit(solution)/shard_map/attend/pallas_call | solution.py:344
  45.2 0.0 copy-start.2
  45.2 12.6 %all_to_all.46 = bf16[8,256,128]{2,1,0:T(8,128)(2,1)S(1)} all-to-all(bf16[8,256,128]{2,1,0:T(8,128)(2,1)S(1)} %bitcast.16), channel_id=1, replica_groups=mesh['far'=4,'near'=8,'head'=8] {'near'}, dimensions={0} | all-to-all | bytes 1048576 | tf_op jit(solution)/shard_map/all_to_all | solution.py:363
  57.8 1.0 %add.5 = bf16[1024,128]{1,0:T(8,128)(2,1)} custom-call(s32[16,32]{1,0:T(8,128)S(4)} %table.1.anc_ref, bf16[2048,128]{1,0:T(8,128)(2,1)S(1)} %bitcast.13), custom_call_target="tpu_custom_call" | custom-call | tf_op jit(solution)/shard_map/add/pallas_call | solution.py:373
  58.9 0.0 copy-done.2
  58.9 9.5 %all-to-all-start.3 = ((bf16[256,4,128]{2,1,0:T(4,128)(2,1)}), bf16[256,4,128]{2,1,0:T(4,128)(2,1)S(1)}, u32[]{:S(2)}, u32[]{:S(2)}) async-start(bf16[256,4,128]{2,1,0:T(4,128)(2,1)} %bitcast.8), calls=%async_computation.3 | async-start | bytes 524288 | tf_op jit(solution)/shard_map/all_to_all | solution.py:385
  68.4 0.0 copy-start.3
  68.4 0.9 %copy-done.3 = bf16[128,1024]{1,0:T(8,128)(2,1)S(1)} copy-done((bf16[128,1024]{1,0:T(8,128)(2,1)S(1)}, bf16[128,1024]{1,0:T(8,128)(2,1)}, u32[]{:S(2)}) %copy-start.3) | copy-done | bytes 262168
  69.3 1.4 %late.1 = (bf16[128,1024]{1,0:T(8,128)(2,1)}, f32[128,1024]{1,0:T(8,128)}) custom-call(s32[16,32]{1,0:T(8,128)S(4)} %table.1.anc_ref, bf16[2048,128]{1,0:T(8,128)(2,1)S(1)} %bitcast.11, bf16[1024,1024]{1,0:T(8,128)(2,1)S(1)} %get-tuple-element.17.dl_ref, bf16[128,1024]{1,0:T(8,128)(2,1)S(1)} %copy-done.3), custom_call_target="tpu_custom_call" | custom-call | tf_op jit(solution)/shard_map/late/pallas_call | solution.py:364
  70.7 13.0 %all-to-all-done.3 = bf16[256,4,128]{2,1,0:T(4,128)(2,1)S(1)} async-done(((bf16[256,4,128]{2,1,0:T(4,128)(2,1)}), bf16[256,4,128]{2,1,0:T(4,128)(2,1)S(1)}, u32[]{:S(2)}, u32[]{:S(2)}) %all-to-all-start.3) | async-done | bytes 262176 | tf_op jit(solution)/shard_map/all_to_all | solution.py:385
  83.6 0.7 finish.1
Async XLA Ops:
  2.1 30.9 %all-to-all-start = ((bf16[256,4,128]{2,1,0:T(4,128)(2,1)}), bf16[256,4,128]{2,1,0:T(4,128)(2,1)S(1)}, u32[]{:S(2)}, u32[]{:S(2)}) async-start(bf16[256,4,128]{2,1,0:T(4,128)(2,1)} %bitcast), calls=%async_computation | async-start | bytes 524288 | tf_op jit(solution)/shard_map/all_to_all | solution.py:323
  17.8 1.0 %copy-start = (bf16[128,1024]{1,0:T(8,128)(2,1)S(1)}, bf16[128,1024]{1,0:T(8,128)(2,1)}, u32[]{:S(2)}) copy-start(bf16[128,1024]{1,0:T(8,128)(2,1)} %q_ref.1) | copy-start | bytes 786436
  18.8 0.9 %copy-start.1 = (bf16[128,1024]{1,0:T(8,128)(2,1)S(1)}, bf16[128,1024]{1,0:T(8,128)(2,1)}, u32[]{:S(2)}) copy-start(bf16[128,1024]{1,0:T(8,128)(2,1)} %g_ref.1) | copy-start | bytes 786436
  45.2 13.7 %copy-start.2 = (bf16[128,1024]{1,0:T(8,128)(2,1)}, bf16[128,1024]{1,0:T(8,128)(2,1)S(1)}, u32[]{:S(2)}) copy-start(bf16[128,1024]{1,0:T(8,128)(2,1)S(1)} %get-tuple-element.18.out_t_ref) | copy-start | bytes 786436
  58.9 24.8 %all-to-all-start.3 = ((bf16[256,4,128]{2,1,0:T(4,128)(2,1)}), bf16[256,4,128]{2,1,0:T(4,128)(2,1)S(1)}, u32[]{:S(2)}, u32[]{:S(2)}) async-start(bf16[256,4,128]{2,1,0:T(4,128)(2,1)} %bitcast.8), calls=%async_computation.3 | async-start | bytes 524288 | tf_op jit(solution)/shard_map/all_to_all | solution.py:385
  68.4 1.0 %copy-start.3 = (bf16[128,1024]{1,0:T(8,128)(2,1)S(1)}, bf16[128,1024]{1,0:T(8,128)(2,1)}, u32[]{:S(2)}) copy-start(bf16[128,1024]{1,0:T(8,128)(2,1)} %copy-done.2) | copy-start | bytes 786436

commit v5 on v4

--- a/solution.py
+++ b/solution.py
@@ -93,7 +93,7 @@
             pltpu.make_async_copy(block, block, sems.at[s]).wait()
 
 
-def add_kernel(anc_ref, terms_ref, out_ref, even_ref, odd_ref):
+def add_kernel(anc_ref, terms_ref, out_hbm, even_ref, odd_ref, out_ref, sems):
     def term(j, s):
         first = (j * ANC + s) * SHARE
         return terms_ref[first : first + SHARE, :].astype(jnp.float32)
@@ -116,8 +116,15 @@
                 here = pl.ds(pl.multiple_of(place * SHARE, SHARE), SHARE)
                 ref[here, :] = ref[here, :] + term(j, s)
 
-    rows = NODES * SHARE
-    out_ref[...] = (even_ref[:rows, :] + odd_ref[:rows, :]).astype(jnp.bfloat16)
+    part = NODES * SHARE // 4
+    copies = []
+    for c in range(4):
+        here = slice(c * part, (c + 1) * part)
+        out_ref[here, :] = (even_ref[here, :] + odd_ref[here, :]).astype(jnp.bfloat16)
+        copies.append(pltpu.make_async_copy(out_ref.at[here, :], out_hbm.at[here, :], sems.at[c]))
+        copies[-1].start()
+    for copy in copies:
+        copy.wait()
 
 
 def finish_kernel(back_ref, key_ref, value_ref):
@@ -372,12 +379,14 @@
     )(table, kv, near_memory(dlogit), near_memory(out_t))
     summed = pl.pallas_call(
         add_kernel,
-        out_shape=pltpu.VMEM((NODES * SHARE, HD), low),
+        out_shape=shaped((NODES * SHARE, HD), low),
         in_specs=[SMEM, VMEM],
-        out_specs=VMEM,
+        out_specs=HBM,
         scratch_shapes=[
             pltpu.VMEM(((NODES + 1) * SHARE, HD), wide),
             pltpu.VMEM(((NODES + 1) * SHARE, HD), wide),
+            pltpu.VMEM((NODES * SHARE, HD), low),
+            pltpu.SemaphoreType.DMA((4,)),
         ],
         compiler_params=room(8),
         name="add",

time: 84.8 us -> 85.1 us (level)
  no operation moved by 1% of the time
where the time goes in v5:
time: 85.1 us; the launch traced here: 84.8 us
  waiting for transfers between devices  25.2 us (30%)
  starting transfers between devices  25.1 us (29%)
  blocking collectives  23.3 us (27%)
  Pallas kernels  7.66 us (9%)
  local copies, waits for them, and re-layouts  2.85 us (3%)
    all_to_all x1, starting transfers between devices, per_device(): lax.all_to_all(pieces, everyone, split_axis=0, concat_axis=0, tiled=True)  15.7 us
    all_to_all x1, blocking collectives, per_device(): lax.all_to_all(terms, 'near', split_axis=0, concat_axis=0, tiled=True)  13 us
    all_to_all x1, waiting for transfers between devices, per_device(): lax.all_to_all(summed, everyone, split_axis=0, concat_axis=0, tiled=True)  13 us
    all_to_all x1, waiting for transfers between devices, per_device(): lax.all_to_all(pieces, everyone, split_axis=0, concat_axis=0, tiled=True)  12.3 us
    all_to_all x1, blocking collectives, per_device(): lax.all_to_all(picked, 'near', split_axis=0, concat_axis=0, tiled=True)  10.3 us
    all_to_all x1, starting transfers between devices, per_device(): lax.all_to_all(summed, everyone, split_axis=0, concat_axis=0, tiled=True)  9.42 us
    unnamed x8, local copies, waits for them, and re-layouts  2.85 us
  transfers between devices with their start and end apart: 2, of which 2 were waited for; matrix products, arithmetic and copies ran while one was open for 0% of the time, Pallas kernels for 3%

profile of v5, /device:TPU:1, one launch (start us, length us, event | category | flops | bytes accessed | tf_op | source)
XLA Modules:
  0.0 84.8 jit_solution(17707285427186467716)
XLA Ops:
  0.6 1.5 %cut.1 = bf16[1024,128]{1,0:T(8,128)(2,1)} custom-call(bf16[16,1024]{1,0:T(8,128)(2,1)} %key_hbm.1, bf16[16,1024]{1,0:T(8,128)(2,1)} %value_hbm.1), custom_call_target="tpu_custom_call" | custom-call | tf_op jit(solution)/shard_map/cut/pallas_call | solution.py:309
  2.1 15.7 %all-to-all-start = ((bf16[256,4,128]{2,1,0:T(4,128)(2,1)}), bf16[256,4,128]{2,1,0:T(4,128)(2,1)S(1)}, u32[]{:S(2)}, u32[]{:S(2)}) async-start(bf16[256,4,128]{2,1,0:T(4,128)(2,1)} %bitcast), calls=%async_computation | async-start | bytes 524288 | tf_op jit(solution)/shard_map/all_to_all | solution.py:330
  17.8 0.0 copy-start
  17.8 0.9 %copy-done = bf16[128,1024]{1,0:T(8,128)(2,1)S(1)} copy-done((bf16[128,1024]{1,0:T(8,128)(2,1)S(1)}, bf16[128,1024]{1,0:T(8,128)(2,1)}, u32[]{:S(2)}) %copy-start) | copy-done | bytes 262168
  18.8 0.0 copy-start.1
  18.8 0.9 %copy-done.1 = bf16[128,1024]{1,0:T(8,128)(2,1)S(1)} copy-done((bf16[128,1024]{1,0:T(8,128)(2,1)S(1)}, bf16[128,1024]{1,0:T(8,128)(2,1)}, u32[]{:S(2)}) %copy-start.1) | copy-done | bytes 262168
  19.7 0.1 prep.1.in_ref
  19.9 1.0 %table.1.anc_ref = s32[16,32]{1,0:T(8,128)S(4)} custom-call(s32[1]{0:T(128)} %bitcast.2.leaf_ref, s32[8,32]{1,0:T(8,128)} %bitcast.17, s32[32]{0:T(128)} %len_ref.1), custom_call_target="tpu_custom_call" | custom-call | tf_op jit(solution)/shard_map/table/pallas_call | solution.py:322
  20.8 12.3 %all-to-all-done = bf16[256,4,128]{2,1,0:T(4,128)(2,1)S(1)} async-done(((bf16[256,4,128]{2,1,0:T(4,128)(2,1)}), bf16[256,4,128]{2,1,0:T(4,128)(2,1)S(1)}, u32[]{:S(2)}, u32[]{:S(2)}) %all-to-all-start) | async-done | bytes 262176 | tf_op jit(solution)/shard_map/all_to_all | solution.py:330
  33.1 0.8 pick.1
  33.9 10.3 %all_to_all.45 = bf16[8,256,128]{2,1,0:T(8,128)(2,1)S(1)} all-to-all(bf16[8,256,128]{2,1,0:T(8,128)(2,1)S(1)} %bitcast.12), channel_id=1, replica_groups=mesh['far'=4,'near'=8,'head'=8] {'near'}, dimensions={0} | all-to-all | bytes 1048576 | tf_op jit(solution)/shard_map/all_to_all | solution.py:350
  44.2 1.1 %attend.1 = (bf16[2048,128]{1,0:T(8,128)(2,1)S(1)}, bf16[1024,1024]{1,0:T(8,128)(2,1)S(1)}, bf16[128,1024]{1,0:T(8,128)(2,1)S(1)}) custom-call(s32[16,32]{1,0:T(8,128)S(4)} %table.1.anc_ref, bf16[3072,128]{1,0:T(8,128)(2,1)S(1)} %prep.1.in_ref, bf16[2048,128]{1,0:T(8,128)(2,1)S(1)} %bitcast.10), custom_call_target="tpu_custom_call" | custom-call | tf_op jit(solution)/shard_map/attend/pallas_call | solution.py:351
  45.3 0.0 copy-start.2
  45.3 13.0 %all_to_all.46 = bf16[8,256,128]{2,1,0:T(8,128)(2,1)S(1)} all-to-all(bf16[8,256,128]{2,1,0:T(8,128)(2,1)S(1)} %bitcast.16), channel_id=1, replica_groups=mesh['far'=4,'near'=8,'head'=8] {'near'}, dimensions={0} | all-to-all | bytes 1048576 | tf_op jit(solution)/shard_map/all_to_all | solution.py:370
  58.4 1.0 %add.5 = bf16[1024,128]{1,0:T(8,128)(2,1)} custom-call(s32[16,32]{1,0:T(8,128)S(4)} %table.1.anc_ref, bf16[2048,128]{1,0:T(8,128)(2,1)S(1)} %bitcast.13), custom_call_target="tpu_custom_call" | custom-call | tf_op jit(solution)/shard_map/add/pallas_call | solution.py:380
  59.4 0.0 copy-done.2
  59.4 9.4 %all-to-all-start.3 = ((bf16[256,4,128]{2,1,0:T(4,128)(2,1)}), bf16[256,4,128]{2,1,0:T(4,128)(2,1)S(1)}, u32[]{:S(2)}, u32[]{:S(2)}) async-start(bf16[256,4,128]{2,1,0:T(4,128)(2,1)} %bitcast.8), calls=%async_computation.3 | async-start | bytes 524288 | tf_op jit(solution)/shard_map/all_to_all | solution.py:394
  68.8 0.0 copy-start.3
  68.9 0.9 %copy-done.3 = bf16[128,1024]{1,0:T(8,128)(2,1)S(1)} copy-done((bf16[128,1024]{1,0:T(8,128)(2,1)S(1)}, bf16[128,1024]{1,0:T(8,128)(2,1)}, u32[]{:S(2)}) %copy-start.3) | copy-done | bytes 262168
  69.8 1.4 %late.1 = (bf16[128,1024]{1,0:T(8,128)(2,1)}, f32[128,1024]{1,0:T(8,128)}) custom-call(s32[16,32]{1,0:T(8,128)S(4)} %table.1.anc_ref, bf16[2048,128]{1,0:T(8,128)(2,1)S(1)} %bitcast.11, bf16[1024,1024]{1,0:T(8,128)(2,1)S(1)} %get-tuple-element.17.dl_ref, bf16[128,1024]{1,0:T(8,128)(2,1)S(1)} %copy-done.3), custom_call_target="tpu_custom_call" | custom-call | tf_op jit(solution)/shard_map/late/pallas_call | solution.py:371
  71.2 13.0 %all-to-all-done.3 = bf16[256,4,128]{2,1,0:T(4,128)(2,1)S(1)} async-done(((bf16[256,4,128]{2,1,0:T(4,128)(2,1)}), bf16[256,4,128]{2,1,0:T(4,128)(2,1)S(1)}, u32[]{:S(2)}, u32[]{:S(2)}) %all-to-all-start.3) | async-done | bytes 262176 | tf_op jit(solution)/shard_map/all_to_all | solution.py:394
  84.1 0.7 finish.1
Async XLA Ops:
  2.1 30.9 %all-to-all-start = ((bf16[256,4,128]{2,1,0:T(4,128)(2,1)}), bf16[256,4,128]{2,1,0:T(4,128)(2,1)S(1)}, u32[]{:S(2)}, u32[]{:S(2)}) async-start(bf16[256,4,128]{2,1,0:T(4,128)(2,1)} %bitcast), calls=%async_computation | async-start | bytes 524288 | tf_op jit(solution)/shard_map/all_to_all | solution.py:330
  17.8 1.0 %copy-start = (bf16[128,1024]{1,0:T(8,128)(2,1)S(1)}, bf16[128,1024]{1,0:T(8,128)(2,1)}, u32[]{:S(2)}) copy-start(bf16[128,1024]{1,0:T(8,128)(2,1)} %q_ref.1) | copy-start | bytes 786436
  18.8 0.9 %copy-start.1 = (bf16[128,1024]{1,0:T(8,128)(2,1)S(1)}, bf16[128,1024]{1,0:T(8,128)(2,1)}, u32[]{:S(2)}) copy-start(bf16[128,1024]{1,0:T(8,128)(2,1)} %g_ref.1) | copy-start | bytes 786436
  45.3 14.1 %copy-start.2 = (bf16[128,1024]{1,0:T(8,128)(2,1)}, bf16[128,1024]{1,0:T(8,128)(2,1)S(1)}, u32[]{:S(2)}) copy-start(bf16[128,1024]{1,0:T(8,128)(2,1)S(1)} %get-tuple-element.18.out_t_ref) | copy-start | bytes 786436
  59.4 24.7 %all-to-all-start.3 = ((bf16[256,4,128]{2,1,0:T(4,128)(2,1)}), bf16[256,4,128]{2,1,0:T(4,128)(2,1)S(1)}, u32[]{:S(2)}, u32[]{:S(2)}) async-start(bf16[256,4,128]{2,1,0:T(4,128)(2,1)} %bitcast.8), calls=%async_computation.3 | async-start | bytes 524288 | tf_op jit(solution)/shard_map/all_to_all | solution.py:394
  68.8 1.0 %copy-start.3 = (bf16[128,1024]{1,0:T(8,128)(2,1)S(1)}, bf16[128,1024]{1,0:T(8,128)(2,1)}, u32[]{:S(2)}) copy-start(bf16[128,1024]{1,0:T(8,128)(2,1)} %copy-done.2) | copy-start | bytes 786436
